TPU v7x, 256 devices: a whole 4x4x8 slice. The times are simulated.
256 devices in a mesh: ctx: 32 (over y, z), tp: 8 (over x, core).
Axes of the slice: x: 4, y: 4, z: 8, core: 2. Of those that a mesh axis runs over, the one named last changes fastest.
Arguments:
- q_in: bfloat16 [8192, 8192], P('ctx', 'tp'), may hold values from -10.5 to 10.5
- k_in: bfloat16 [8192, 8192], P('ctx', 'tp'), may hold values from -6 to 6
- v_in: bfloat16 [8192, 8192], P('ctx', 'tp'), may hold values from -6 to 6
- grad_out: bfloat16 [8192, 8192], P('ctx', 'tp'), may hold values from -6 to 6
- doc_ids: int32 [8192], P('ctx'), may hold values from 0 to 3, never falling along the last dimension, each value on 1 to 4096 neighbouring positions
- gain: bfloat16 [8192], P('tp'), may hold values from 0.099609375 to 1.8984375
- filters: bfloat16 [512, 128], P('tp'), may hold values from -0.5 to 0.5
- short_weight: bfloat16 [3, 3, 8192], P(None, None, 'tp'), may hold values from -3.5 to 3.5
Outputs:
- grad_q: bfloat16 [8192, 8192], P('ctx', 'tp')
- grad_k: bfloat16 [8192, 8192], P('ctx', 'tp')
- grad_v: bfloat16 [8192, 8192], P('ctx', 'tp')
- grad_gain: float32 [8192], P('tp')
- grad_filters: float32 [512, 128], P('tp')
- grad_short: float32 [3, 3, 8192], P(None, None, 'tp')
Inputs may be any that keep to these rules, and one draw needn't show every extreme that they name: doc_ids never fall along the window, so every document is one run of consecutive tokens; one document covers exactly 4096 tokens.
All inputs are finite; a program needn't handle non-finite values.
Results may differ from a plain program's by a relative error of at most 0.0049.
Values may be sent and summed in bfloat16 or wider, within the bound.
A program may use at most 128 MiB of HBM per device.

v0:
```python
import math

import jax
import jax.numpy as jnp
from jax import lax
from jax.sharding import PartitionSpec as P

D = 8192


EPS = 1e-06


def shifted(value, axis, by):
    count = lax.axis_size(axis)
    pairs = [(i, i + by) for i in range(count) if 0 <= i + by < count]
    return lax.ppermute(value, axis, pairs)


def featurize(extended, weights, marks_ext, rim_edge):
    length = extended.shape[0] - rim_edge
    own_marks = marks_ext[rim_edge:]
    running = jnp.zeros((length, extended.shape[1]), jnp.float32)
    for offset in range(rim_edge + 1):
        start_row = rim_edge - offset
        agree = (marks_ext[start_row : start_row + length] == own_marks).astype(jnp.float32)[
            :, None
        ]
        running = (
            running
            + weights[offset].astype(jnp.float32)[None, :]
            * extended[start_row : start_row + length].astype(jnp.float32)
            * agree
        )
    return running


def banded(coeffs, block_rows):
    groups, taps = coeffs.shape
    span_cols = block_rows + taps - 1
    padded = jnp.concatenate([coeffs, jnp.zeros((groups, block_rows), coeffs.dtype)], axis=1)
    repeated = jnp.tile(padded, (1, block_rows))[:, : block_rows * span_cols]
    return repeated.reshape(groups, block_rows, span_cols)


def diagonal_sums(pair_grad, taps):
    groups, block_rows, span_cols = pair_grad.shape
    flat_terms = pair_grad.reshape(groups, block_rows * span_cols)
    flat_terms = jnp.concatenate([flat_terms, jnp.zeros((groups, block_rows), jnp.float32)], axis=1)
    return jnp.sum(flat_terms.reshape(groups, block_rows, span_cols + 1)[:, :, :taps], axis=1)


def unfeature(grad_feat, tail, weights, marks_after, own_marks):
    row_count = grad_feat.shape[0]
    extended = jnp.concatenate([grad_feat, tail], axis=0)
    running = jnp.zeros(grad_feat.shape, jnp.float32)
    for offset in range(weights.shape[0]):
        agree = (marks_after[offset : offset + row_count] == own_marks).astype(jnp.float32)[:, None]
        running = (
            running
            + weights[offset].astype(jnp.float32)[None, :]
            * extended[offset : offset + row_count]
            * agree
        )
    return running.astype(jnp.bfloat16)


def short_terms(grad_feat, short_in, short_marks, own_marks, rim_edge):
    row_count = grad_feat.shape[0]
    pieces = []
    for offset in range(rim_edge + 1):
        start_row = rim_edge - offset
        agree = (short_marks[start_row : start_row + row_count] == own_marks).astype(jnp.float32)[
            :, None
        ]
        pieces.append(
            jnp.sum(
                grad_feat * short_in[start_row : start_row + row_count].astype(jnp.float32) * agree,
                axis=0,
            )
        )
    return jnp.stack(pieces)


def on_device(q_in, k_in, v_in, grad_out, doc_ids, gain, filters, short_weight):
    row_count, channels = q_in.shape
    groups, taps = filters.shape
    group_width = channels // groups
    rim_edge = short_weight.shape[1] - 1
    tap_reach = taps - 1
    rim_span = tap_reach + rim_edge
    block_rows = min(row_count, max(128, row_count // 8))
    span_cols = block_rows + tap_reach
    grad_scale = 1.0 / math.sqrt(row_count * lax.axis_size("ctx"))
    doc_marks = doc_ids + 1
    previous = shifted(
        (
            q_in[row_count - rim_edge :],
            k_in[row_count - rim_span :],
            v_in[row_count - rim_span :],
            doc_marks[row_count - rim_span :],
        ),
        "ctx",
        1,
    )
    marks_ext = jnp.concatenate([previous[3], doc_marks], axis=0)
    long_marks = marks_ext[rim_edge:]
    short_marks = marks_ext[tap_reach:]
    q_short = jnp.concatenate([previous[0], q_in], axis=0)
    k_ext = jnp.concatenate([previous[1], k_in], axis=0)
    v_ext = jnp.concatenate([previous[2], v_in], axis=0)
    k_short = k_ext[tap_reach:]
    v_short = v_ext[tap_reach:]
    k_wide = featurize(k_ext, short_weight[1], marks_ext, rim_edge)
    v_wide = featurize(v_ext, short_weight[2], marks_ext, rim_edge)
    product_ext = (k_wide * v_wide).astype(jnp.bfloat16)
    feat_k = k_wide[tap_reach:]
    feat_v = v_wide[tap_reach:]
    feat_q = featurize(q_short, short_weight[0], short_marks, rim_edge)
    forward_band = banded(filters[:, ::-1], block_rows)
    backward_band = banded(filters, block_rows)
    masks = []
    mixed_parts = []
    for start in range(0, row_count, block_rows):
        agree = (
            long_marks[start : start + span_cols][None, :]
            == doc_marks[start : start + block_rows][:, None]
        ).astype(jnp.bfloat16)
        masks.append(agree)
        segment = product_ext[start : start + span_cols].reshape(span_cols, groups, group_width)
        mixed_parts.append(
            jnp.einsum(
                "gij,jgc->igc",
                forward_band * agree[None],
                segment,
                preferred_element_type=jnp.float32,
            ).reshape(block_rows, channels)
        )
    mixed = jnp.concatenate(mixed_parts, axis=0)
    y_out = feat_q * mixed
    weighted = gain.astype(jnp.float32)[None, :] * grad_out.astype(jnp.float32)
    square_sum, inner_sum = lax.psum(
        (jnp.sum(y_out * y_out, axis=1), jnp.sum(weighted * y_out, axis=1)), "tp"
    )
    row_scale = lax.rsqrt(square_sum / D + EPS)
    grad_y = row_scale[:, None] * weighted - y_out * (row_scale**3 * inner_sum / D)[:, None]
    gain_term = (
        jnp.sum(grad_out.astype(jnp.float32) * y_out * row_scale[:, None], axis=0) * grad_scale
    )
    grad_gain = lax.psum(gain_term, "ctx")
    grad_fq = grad_y * mixed
    grad_mixed = (grad_y * feat_q).astype(jnp.bfloat16)
    following = shifted((grad_mixed[:tap_reach], doc_marks[:tap_reach]), "ctx", -1)
    mixed_ext = jnp.concatenate([grad_mixed, following[0]], axis=0)
    marks_after = jnp.concatenate([doc_marks, following[1]], axis=0)
    prod_parts = []
    filter_term = jnp.zeros((groups, taps), jnp.float32)
    for position, start in enumerate(range(0, row_count, block_rows)):
        agree = (
            marks_after[start : start + span_cols][None, :]
            == doc_marks[start : start + block_rows][:, None]
        ).astype(jnp.bfloat16)
        segment = mixed_ext[start : start + span_cols].reshape(span_cols, groups, group_width)
        prod_parts.append(
            jnp.einsum(
                "gij,jgc->igc",
                backward_band * agree[None],
                segment,
                preferred_element_type=jnp.float32,
            ).reshape(block_rows, channels)
        )
        own_block = grad_mixed[start : start + block_rows].reshape(block_rows, groups, group_width)
        behind = product_ext[start : start + span_cols].reshape(span_cols, groups, group_width)
        pair_grad = (
            jnp.einsum("igc,jgc->gij", own_block, behind, preferred_element_type=jnp.float32)
            * masks[position].astype(jnp.float32)[None]
        )
        filter_term = filter_term + diagonal_sums(pair_grad, taps)
    filter_term = filter_term[:, ::-1] * grad_scale
    grad_filters = lax.psum(filter_term, "ctx")
    grad_prod = jnp.concatenate(prod_parts, axis=0)
    grad_fk = grad_prod * feat_v
    grad_fv = grad_prod * feat_k
    tails_after = shifted(
        jnp.stack([grad_fq[:rim_edge], grad_fk[:rim_edge], grad_fv[:rim_edge]]), "ctx", -1
    )
    grad_q = unfeature(grad_fq, tails_after[0], short_weight[0], marks_after, doc_marks)
    grad_k = unfeature(grad_fk, tails_after[1], short_weight[1], marks_after, doc_marks)
    grad_v = unfeature(grad_fv, tails_after[2], short_weight[2], marks_after, doc_marks)
    short_term = (
        jnp.stack(
            [
                short_terms(grad_fq, q_short, short_marks, doc_marks, rim_edge),
                short_terms(grad_fk, k_short, short_marks, doc_marks, rim_edge),
                short_terms(grad_fv, v_short, short_marks, doc_marks, rim_edge),
            ]
        )
        * grad_scale
    )
    grad_short = lax.psum(short_term, "ctx")
    return (grad_q, grad_k, grad_v, grad_gain, grad_filters, grad_short)


def solution(mesh):
    return jax.shard_map(
        on_device,
        mesh=mesh,
        in_specs=(
            P("ctx", "tp"),
            P("ctx", "tp"),
            P("ctx", "tp"),
            P("ctx", "tp"),
            P("ctx"),
            P("tp"),
            P("tp", None),
            P(None, None, "tp"),
        ),
        out_specs=(
            P("ctx", "tp"),
            P("ctx", "tp"),
            P("ctx", "tp"),
            P("tp"),
            P("tp", None),
            P(None, None, "tp"),
        ),
        check_vma=False,
    )
```

profile of v0, /device:TPU:2, one launch (start us, length us, event | category | flops | bytes accessed | tf_op | source)
XLA Modules:
  0.0 352.5 jit_solution(16350759475145604191)
XLA Ops:
  8.2 3.8 %collective-permute-start.3 = (bf16[129,1024]{1,0:T(8,128)(2,1)S(1)}, bf16[129,1024]{1,0:T(8,128)(2,1)S(1)}, u32[]{:S(2)}, u32[]{:S(2)}) collective-permute-start(bf16[129,1024]{1,0:T(8,128)(2,1)S(1)} %slice.289), channel_id=1, source_target_pairs={{0,8},{8,16},{16,24},{24,32},{32,40},{40,48},{48,56},{56,64},{64,7... | collective-permute-start | bytes 792584 | tf_op jit(solution)/shard_map/ppermute | solution.py:17
  14.1 4.5 %collective-permute-start.1 = (s32[129]{0:T(256)S(1)}, s32[129]{0:T(256)S(1)}, u32[]{:S(2)}, u32[]{:S(2)}) collective-permute-start(s32[129]{0:T(256)S(1)} %slice.273), channel_id=1, source_target_pairs={{0,8},{8,16},{16,24},{24,32},{32,40},{40,48},{48,56},{56,64},{64,7... | collective-permute-start | bytes 1556 | tf_op jit(solution)/shard_map/ppermute | solution.py:17
  20.0 4.4 %collective-permute-start = (bf16[2,1024]{1,0:T(2,128)(2,1)}, bf16[2,1024]{1,0:T(2,128)(2,1)}, u32[]{:S(2)}, u32[]{:S(2)}) collective-permute-start(bf16[2,1024]{1,0:T(2,128)(2,1)} %slice.271), channel_id=1, source_target_pairs={{0,8},{8,16},{16,24},{24,32},{32,40},{40,48},{48,56},{56,64},{64,7... | collective-permute-start | bytes 12296 | tf_op jit(solution)/shard_map/ppermute | solution.py:17
  25.4 4.4 %collective-permute-start.2 = (bf16[129,1024]{1,0:T(8,128)(2,1)S(1)}, bf16[129,1024]{1,0:T(8,128)(2,1)S(1)}, u32[]{:S(2)}, u32[]{:S(2)}) collective-permute-start(bf16[129,1024]{1,0:T(8,128)(2,1)S(1)} %slice.279), channel_id=1, source_target_pairs={{0,8},{8,16},{16,24},{24,32},{32,40},{40,48},{48,56},{56,64},{64,7... | collective-permute-start | bytes 792584 | tf_op jit(solution)/shard_map/ppermute | solution.py:17
  33.2 2.6 copy.34
  38.1 16.1 %reshape.317 = bf16[64,128,255]{2,1,0:T(8,128)(2,1)} reshape(bf16[64,32640]{1,0:T(8,128)(2,1)} %slice.348) | data formatting | bytes 8355840 | tf_op jit(solution)/shard_map/reshape | solution.py:43
  55.1 2.6 copy.35
  60.0 15.9 %reshape.322 = bf16[64,128,255]{2,1,0:T(8,128)(2,1)} reshape(bf16[64,32640]{1,0:T(8,128)(2,1)} %slice.352) | data formatting | bytes 8355840 | tf_op jit(solution)/shard_map/reshape | solution.py:43
  77.7 5.0 %multiply_convert_fusion = (bf16[383,1024]{1,0:T(8,128)(2,1)S(1)}, f32[383,1024]{1,0:T(8,128)}, f32[383,1024]{1,0:T(8,128)}) fusion(f32[383]{0:T(512)S(1)} %get-tuple-element.56, f32[1024]{0:T(1024)S(1)} %bitcast.107, f32[383]{0:T(512)S(1)} %get-tuple-element.55, f32[1024]{0:T(1024)S(1)} %bitcast.109, bf16[256,1024]{1,0:T(8,128)(2,1)S(1)} %copy-done.13, ...), kind=kLoop, calls=%fused_computation.16 | loop fusion | flops 15687680 | bytes 5526520 | tf_op jit(solution)/shard_map/convert_element_type | solution.py:116
  83.3 3.6 %fusion.4 = f32[64,16,128]{2,1,0:T(8,128)S(1)} fusion(bf16[255,64,16]{0,2,1:T(8,128)(2,1)S(1)} %bitcast.78, bf16[64,128,255]{2,1,0:T(8,128)(2,1)} %reshape.317, bf16[128,255]{1,0:T(8,128)(2,1)S(1)} %get-tuple-element.70), kind=kOutput, calls=%fused_computation.8 | convolution fusion | flops 68935680 | bytes 5289728 | tf_op jit(solution)/shard_map/gij,jgc->igc/dot_general | solution.py:132
  91.2 10.7 %psum.35 = f32[256]{0:T(256)S(1)} all-reduce(f32[256]{0:T(256)} %get-tuple-element.26), channel_id=1, replica_groups=mesh['ctx'=32,'tp'=8] {'tp'}, use_global_device_ids=true, to_apply=%region_1.0 | all-reduce | flops 256 | bytes 2048 | tf_op jit(solution)/shard_map/psum | solution.py:142
  103.5 12.4 %psum.36 = f32[256]{0:T(256)S(1)} all-reduce(f32[256]{0:T(256)S(1)} %get-tuple-element.16), channel_id=1, replica_groups=mesh['ctx'=32,'tp'=8] {'tp'}, use_global_device_ids=true, to_apply=%region_3.0 | all-reduce | flops 256 | bytes 2048 | tf_op jit(solution)/shard_map/psum | solution.py:142
  122.6 5.5 %broadcast_multiply_fusion.1 = f32[64,128,255]{2,1,0:T(8,128)} fusion(f32[128,255]{1,0:T(8,128)} %get-tuple-element.59, bf16[128,64,16]{0,2,1:T(8,128)(2,1)} %bitcast.88, bf16[255,64,16]{0,2,1:T(8,128)(2,1)S(1)} %bitcast.81), kind=kOutput, calls=%fused_computation.3 | convolution fusion | flops 68935680 | bytes 9270784 | tf_op jit(solution)/shard_map/igc,jgc->gij/dot_general | solution.py:175
  128.1 9.4 %reshape.327 = f32[64,32640]{1,0:T(8,128)} reshape(f32[64,128,255]{2,1,0:T(8,128)} %broadcast_multiply_fusion.1) | data formatting | bytes 16711680 | tf_op jit(solution)/shard_map/reshape | solution.py:48
  137.5 4.0 %concatenate.58 = f32[64,32768]{1,0:T(8,128)S(1)} pad(f32[64,32640]{1,0:T(8,128)} %reshape.327, f32[]{:T(128)} %constant.19.clone.1), padding=0_0x0_128 | pad | bytes 16744452 | tf_op jit(solution)/shard_map/concatenate | solution.py:49
  147.0 5.5 %broadcast_multiply_fusion = f32[64,128,255]{2,1,0:T(8,128)} fusion(f32[128,255]{1,0:T(8,128)S(1)} %get-tuple-element.71, bf16[128,64,16]{0,2,1:T(8,128)(2,1)} %bitcast.89, bf16[255,64,16]{0,2,1:T(8,128)(2,1)S(1)} %bitcast.79), kind=kOutput, calls=%fused_computation.2 | convolution fusion | flops 68935680 | bytes 9270784 | tf_op jit(solution)/shard_map/igc,jgc->gij/dot_general | solution.py:175
  152.5 9.4 %reshape.330 = f32[64,32640]{1,0:T(8,128)} reshape(f32[64,128,255]{2,1,0:T(8,128)} %broadcast_multiply_fusion) | data formatting | bytes 16711680 | tf_op jit(solution)/shard_map/reshape | solution.py:48
  162.0 4.0 %concatenate.59 = f32[64,32768]{1,0:T(8,128)S(1)} pad(f32[64,32640]{1,0:T(8,128)} %reshape.330, f32[]{:T(128)} %constant.19.clone.1), padding=0_0x0_128 | pad | bytes 16744452 | tf_op jit(solution)/shard_map/concatenate | solution.py:49
  173.7 4.2 %fusion = f32[64,16,128]{2,1,0:T(8,128)} fusion(bf16[255,64,16]{0,2,1:T(8,128)(2,1)S(1)} %bitcast.86, bf16[64,128,255]{2,1,0:T(8,128)(2,1)} %reshape.322, bf16[128,255]{1,0:T(8,128)(2,1)S(1)} %copy-done.19), kind=kOutput, calls=%fused_computation.4 | convolution fusion | flops 68935680 | bytes 5289728 | tf_op jit(solution)/shard_map/gij,jgc->igc/dot_general | solution.py:165
  180.2 4.4 %fusion.2 = f32[64,16,128]{2,1,0:T(8,128)} fusion(bf16[255,64,16]{0,2,1:T(8,128)(2,1)} %bitcast.84, bf16[64,128,255]{2,1,0:T(8,128)(2,1)} %reshape.322, bf16[128,255]{1,0:T(8,128)(2,1)S(1)} %copy-done.18), kind=kOutput, calls=%fused_computation.6 | convolution fusion | flops 68935680 | bytes 5289728 | tf_op jit(solution)/shard_map/gij,jgc->igc/dot_general | solution.py:165
  185.9 4.1 %multiply_reduce_fusion.1 = (f32[1024]{0:T(1024)S(1)}, f32[1024]{0:T(1024)S(1)}, f32[1024]{0:T(1024)S(1)}, f32[1024]{0:T(1024)S(1)}, f32[1024]{0:T(1024)S(1)}, /...) fusion(bf16[256,1024]{1,0:T(8,128)(2,1)} %param.10, ...), kind=kLoop, calls=%fused_computation.88 | loop fusion | flops 11266048 | bytes 8165376 | tf_op jit(solution)/shard_map/reduce_sum | solution.py:77
  193.3 5.2 %collective-permute-done.6 = f32[3,2,1024]{2,1,0:T(2,128)S(1)} collective-permute-done((f32[3,2,1024]{2,1,0:T(2,128)S(1)}, f32[3,2,1024]{2,1,0:T(2,128)S(1)}, u32[]{:S(2)}, u32[]{:S(2)}) %collective-permute-start.6) | collective-permute-done | bytes 24608 | tf_op jit(solution)/shard_map/ppermute | solution.py:17
  198.7 4.0 %fusion.19 = (bf16[256,1024]{1,0:T(8,128)(2,1)}, bf16[256,1024]{1,0:T(8,128)(2,1)}) fusion(f32[256,1024]{1,0:T(8,128)} %copy-done.12, f32[2,1024]{1,0:T(2,128)S(1)} %get-tuple-element.37, f32[1024]{0:T(1024)S(1)} %bitcast.108, f32[1024]{0:T(1024)S(1)} %bitcast.110, f32[1024]{0:T(1024)S(1)} %bitcast.100, f32[256]{0:T(256)S(1)} %copy-done.45, ...), kind=kLoop, calls=%fused_computation.48 | loop fusion | flops 5242880 | bytes 3188736 | tf_op jit(solution)/shard_map/convert_element_type | solution.py:65
  203.9 137.5 %all-reduce.7.cloned.1.call-done = (f32[1024]{0:T(1024)}, f32[64,128]{1,0:T(8,128)}, f32[3,3,1024]{2,1,0:T(4,128)}) async-done(((f32[1024]{0:T(1024)}, f32[64,128]{1,0:T(8,128)}, f32[3,3,1024]{2,1,0:T(4,128)}), (f32[1024]{0:T(1024)}, f32[64,128]{1,0:T(8,128)}, f32[3,3,1024]{2,1,0:T(4,128)})) %all-reduce.7.cloned.1.call-update) | async-done | bytes 73744 | tf_op jit(solution)/shard_map/psum | solution.py:150
  (173 shorter events, 54.2 us)
Async XLA Ops:
  7.2 334.2 %all-reduce.7.cloned.1.call-start = ((), (), s32[]{:S(2)}) async-start(), calls=%async_computation | async-start | bytes 172032 | tf_op jit(solution)/shard_map/psum | solution.py:150
  8.2 69.4 %collective-permute-start.3 = (bf16[129,1024]{1,0:T(8,128)(2,1)S(1)}, bf16[129,1024]{1,0:T(8,128)(2,1)S(1)}, u32[]{:S(2)}, u32[]{:S(2)}) collective-permute-start(bf16[129,1024]{1,0:T(8,128)(2,1)S(1)} %slice.289), channel_id=1, source_target_pairs={{0,8},{8,16},{16,24},{24,32},{32,40},{40,48},{48,56},{56,64},{64,7... | collective-permute-start | bytes 792584 | tf_op jit(solution)/shard_map/ppermute | solution.py:17
  12.8 63.1 %collective-permute-start.5 = (s32[127]{0:T(128)S(1)}, s32[127]{0:T(128)S(1)}, u32[]{:S(2)}, u32[]{:S(2)}) collective-permute-start(s32[127]{0:T(128)S(1)} %slice.308), channel_id=1, source_target_pairs={{8,0},{16,8},{24,16},{32,24},{40,32},{48,40},{56,48},{64,56},{72,6... | collective-permute-start | bytes 1532 | tf_op jit(solution)/shard_map/ppermute | solution.py:17
  14.1 61.7 %collective-permute-start.1 = (s32[129]{0:T(256)S(1)}, s32[129]{0:T(256)S(1)}, u32[]{:S(2)}, u32[]{:S(2)}) collective-permute-start(s32[129]{0:T(256)S(1)} %slice.273), channel_id=1, source_target_pairs={{0,8},{8,16},{16,24},{24,32},{32,40},{40,48},{48,56},{56,64},{64,7... | collective-permute-start | bytes 1556 | tf_op jit(solution)/shard_map/ppermute | solution.py:17
  20.0 68.6 %collective-permute-start = (bf16[2,1024]{1,0:T(2,128)(2,1)}, bf16[2,1024]{1,0:T(2,128)(2,1)}, u32[]{:S(2)}, u32[]{:S(2)}) collective-permute-start(bf16[2,1024]{1,0:T(2,128)(2,1)} %slice.271), channel_id=1, source_target_pairs={{0,8},{8,16},{16,24},{24,32},{32,40},{40,48},{48,56},{56,64},{64,7... | collective-permute-start | bytes 12296 | tf_op jit(solution)/shard_map/ppermute | solution.py:17
  25.4 52.2 %collective-permute-start.2 = (bf16[129,1024]{1,0:T(8,128)(2,1)S(1)}, bf16[129,1024]{1,0:T(8,128)(2,1)S(1)}, u32[]{:S(2)}, u32[]{:S(2)}) collective-permute-start(bf16[129,1024]{1,0:T(8,128)(2,1)S(1)} %slice.279), channel_id=1, source_target_pairs={{0,8},{8,16},{16,24},{24,32},{32,40},{40,48},{48,56},{56,64},{64,7... | collective-permute-start | bytes 792584 | tf_op jit(solution)/shard_map/ppermute | solution.py:17
  31.4 46.2 %copy-start.25 = (f32[1,1,1024]{2,1,0:T(1,128)}, f32[1,1,1024]{2,1,0:T(1,128)S(1)}, u32[]{:S(2)}) copy-start(f32[1,1,1024]{2,1,0:T(1,128)S(1)} %get-tuple-element.41) | copy-start | bytes 12292
  31.4 46.2 %copy-start.27 = (f32[1,1,1024]{2,1,0:T(1,128)}, f32[1,1,1024]{2,1,0:T(1,128)S(1)}, u32[]{:S(2)}) copy-start(f32[1,1,1024]{2,1,0:T(1,128)S(1)} %get-tuple-element.42) | copy-start | bytes 12292
  31.4 46.2 %copy-start.29 = (f32[1,1,1024]{2,1,0:T(1,128)}, f32[1,1,1024]{2,1,0:T(1,128)S(1)}, u32[]{:S(2)}) copy-start(f32[1,1,1024]{2,1,0:T(1,128)S(1)} %get-tuple-element.43) | copy-start | bytes 12292
  31.4 46.2 %copy-start.31 = (f32[1,1,1024]{2,1,0:T(1,128)}, f32[1,1,1024]{2,1,0:T(1,128)S(1)}, u32[]{:S(2)}) copy-start(f32[1,1,1024]{2,1,0:T(1,128)S(1)} %get-tuple-element.44) | copy-start | bytes 12292
  31.4 46.2 %copy-start.33 = (f32[1,1,1024]{2,1,0:T(1,128)}, f32[1,1,1024]{2,1,0:T(1,128)S(1)}, u32[]{:S(2)}) copy-start(f32[1,1,1024]{2,1,0:T(1,128)S(1)} %get-tuple-element.47) | copy-start | bytes 12292
  31.4 46.2 %copy-start.35 = (f32[1,1,1024]{2,1,0:T(1,128)}, f32[1,1,1024]{2,1,0:T(1,128)S(1)}, u32[]{:S(2)}) copy-start(f32[1,1,1024]{2,1,0:T(1,128)S(1)} %get-tuple-element.48) | copy-start | bytes 12292
  38.1 16.1 %copy-start.47 = (bf16[1024]{0:T(1024)(128)(2,1)S(1)}, bf16[1024]{0:T(1024)(128)(2,1)}, u32[]{:S(2)}) copy-start(bf16[1024]{0:T(1024)(128)(2,1)} %param.13) | copy-start | bytes 6148
  60.0 16.0 %copy-start.46 = (s32[256]{0:T(256)S(1)}, s32[256]{0:T(256)}, u32[]{:S(2)}) copy-start(s32[256]{0:T(256)} %param.12) | copy-start | bytes 3076
  60.0 17.7 %copy-start.13 = (bf16[256,1024]{1,0:T(8,128)(2,1)S(1)}, bf16[256,1024]{1,0:T(8,128)(2,1)}, u32[]{:S(2)}) copy-start(bf16[256,1024]{1,0:T(8,128)(2,1)} %param.10) | copy-start | bytes 1572868
  60.0 17.7 %copy-start.14 = (bf16[256,1024]{1,0:T(8,128)(2,1)S(1)}, bf16[256,1024]{1,0:T(8,128)(2,1)}, u32[]{:S(2)}) copy-start(bf16[256,1024]{1,0:T(8,128)(2,1)} %param.9) | copy-start | bytes 1572868
  88.5 14.9 %copy-start.4 = (f32[128,1024]{1,0:T(8,128)}, f32[128,1024]{1,0:T(8,128)S(1)}, u32[]{:S(2)}) copy-start(f32[128,1024]{1,0:T(8,128)S(1)} %copy.26) | copy-start | bytes 1572868
  88.5 13.3 %copy-start.2 = (bf16[256,1024]{1,0:T(8,128)(2,1)S(1)}, bf16[256,1024]{1,0:T(8,128)(2,1)}, u32[]{:S(2)}) copy-start(bf16[256,1024]{1,0:T(8,128)(2,1)} %param.11) | copy-start | bytes 1572868
  101.8 14.0 %copy-start.39 = (f32[256]{0:T(256)}, f32[256]{0:T(256)S(1)}, u32[]{:S(2)}) copy-start(f32[256]{0:T(256)S(1)} %add_rsqrt_fusion) | copy-start | bytes 3076
  119.5 51.0 %collective-permute-start.4 = (bf16[127,1024]{1,0:T(8,128)(2,1)}, bf16[127,1024]{1,0:T(8,128)(2,1)}, u32[]{:S(2)}, u32[]{:S(2)}) collective-permute-start(bf16[127,1024]{1,0:T(8,128)(2,1)} %slice.353), channel_id=1, source_target_pairs={{8,0},{16,8},{24,16},{32,24},{40,32},{48,40},{56,48},{64,56},{72,6... | collective-permute-start | bytes 780296 | tf_op jit(solution)/shard_map/ppermute | solution.py:17
  190.0 8.6 %copy-start.26 = (f32[1,1,1024]{2,1,0:T(1,128)S(1)}, f32[1,1,1024]{2,1,0:T(1,128)}, u32[]{:S(2)}) copy-start(f32[1,1,1024]{2,1,0:T(1,128)} %copy-done.25) | copy-start | bytes 12292
  190.0 8.5 %copy-start.28 = (f32[1,1,1024]{2,1,0:T(1,128)S(1)}, f32[1,1,1024]{2,1,0:T(1,128)}, u32[]{:S(2)}) copy-start(f32[1,1,1024]{2,1,0:T(1,128)} %copy-done.27) | copy-start | bytes 12292
  190.0 8.5 %copy-start.30 = (f32[1,1,1024]{2,1,0:T(1,128)S(1)}, f32[1,1,1024]{2,1,0:T(1,128)}, u32[]{:S(2)}) copy-start(f32[1,1,1024]{2,1,0:T(1,128)} %copy-done.29) | copy-start | bytes 12292
  191.3 7.3 %collective-permute-start.6 = (f32[3,2,1024]{2,1,0:T(2,128)S(1)}, f32[3,2,1024]{2,1,0:T(2,128)S(1)}, u32[]{:S(2)}, u32[]{:S(2)}) collective-permute-start(f32[3,2,1024]{2,1,0:T(2,128)S(1)} %pad_maximum_fusion.9), channel_id=1, source_target_pairs={{8,0},{16,8},{24,16},{32,24},{40,32},{48,40},{56,48},{64,56},{72,6... | collective-permute-start | bytes 73736 | tf_op jit(solution)/shard_map/ppermute | solution.py:17
  (32 other events, 137.5 us)
Sparse Core Ops, SparseCore 0:
  193.5 147.8 all-reduce.6
where the time goes:
time: 357 us; the launch traced here: 353 us
  waiting for transfers between devices  143 us (40%)
  local copies, waits for them, and re-layouts  96.4 us (27%)
  other arithmetic  29.8 us (8%)
  matrix products  24.4 us (7%)
  blocking collectives  23.1 us (6%)
  starting transfers between devices  21 us (6%)
  between operations  15.1 us (4%)
    psum x1, waiting for transfers between devices, on_device(): grad_gain = lax.psum(gain_term, 'ctx')  137 us
    reshape x2, local copies, waits for them, and re-layouts, banded(): return repeated.reshape(groups, block_rows, span_cols)  32 us
    psum x2, blocking collectives, on_device(): lax.psum((jnp.sum(y_out * y_out, axis=1), jnp.sum(weighted * y_out, axis=...  23.1 us
    ppermute x7, starting transfers between devices, shifted(): return lax.ppermute(value, axis, pairs)  21 us
    reshape x2, local copies, waits for them, and re-layouts, diagonal_sums(): flat_terms = pair_grad.reshape(groups, block_rows * span_cols)  18.8 us
    unnamed x103, local copies, waits for them, and re-layouts  16.4 us
    dot_general x2, matrix products, on_device(): jnp.einsum('igc,jgc->gij', own_block, behind, preferred_element_type=jnp....  11 us
    dot_general x2, matrix products, on_device(): jnp.einsum('gij,jgc->igc', backward_band * agree[None], segment, preferre...  8.53 us
  transfers between devices with their start and end apart: 8, of which 2 were waited for; matrix products, arithmetic and copies ran while one was open for 33% of the time, Pallas kernels for 0%

commit v1 on v0

v1 whole, which is shorter than its diff:
```python
import functools
import math

import jax
import jax.numpy as jnp
from jax import lax
from jax.experimental import pallas as pl
from jax.experimental.pallas import tpu as pltpu
from jax.sharding import PartitionSpec as P

F32 = jnp.float32
BF16 = jnp.bfloat16
MESH = pl.DeviceIdType.MESH
LANES = 128
HALF = 128
ROWS = 256
SHORT = 3
EPS = 1e-06
RING = 8
CHUNK = 24


def iota(axis):
    return lax.broadcasted_iota(jnp.int32, (LANES, LANES), axis)


def as_column(row, flipped=False):
    eye = flip() if flipped else iota(0) == iota(1)
    spread = jnp.where(eye, jnp.broadcast_to(row, (LANES, LANES)), 0.0)
    return jnp.sum(spread, axis=1, keepdims=True)


def flip():
    return iota(0) + iota(1) == LANES - 1


def mirror():
    total = iota(0) + iota(1)
    return jnp.where((total == 0) | (total == LANES), 1.0, 0.0)


def kernel(
    ny,
    nz,
    ntp,
    q_hbm,
    k_hbm,
    v_hbm,
    go_hbm,
    docs_ref,
    gain_ref,
    filt_ref,
    sw_ref,
    gq_hbm,
    gk_hbm,
    gv_hbm,
    gain_out,
    filt_out,
    short_out,
    xin,
    go_v,
    xf,
    feats,
    mixed,
    y_s,
    grads,
    outs,
    prod,
    gmix,
    tf,
    tb,
    fmask,
    bmask,
    fmask32,
    filt32,
    filt_rev,
    wsc,
    dcol,
    m1,
    m2,
    docs_prev,
    docs_next,
    edge_s,
    edge_r,
    tail_s,
    tail_r,
    acc,
    stats,
    scales,
    big,
    small,
    lhs_s,
    red,
    red_a,
    red_b,
    fin,
    load_sem,
    store_sem,
    doc_sem,
    edge_sem,
    h1_send,
    h1_recv,
    h2_send,
    h2_recv,
    st_send,
    st_recv,
    ra_send,
    ra_recv,
    rb_send,
    rb_recv,
    rc_send,
    rc_recv,
):
    nt = nz
    groups = filt_ref.shape[0]
    per_tile = groups // nt
    width = LANES // per_tile
    n_ctx = ny * nz
    channels = nt * LANES
    total_channels = channels * ntp
    grad_scale = 1.0 / math.sqrt(ROWS * n_ctx)
    ctx = lax.axis_index("ctx")
    tp = lax.axis_index("tp")
    nxt = lax.rem(ctx + 1, n_ctx)
    prv = lax.rem(ctx + n_ctx - 1, n_ctx)
    y_at = lax.div(ctx, nz)
    z_at = lax.rem(ctx, nz)

    def z_peer(d):
        return lax.rem(z_at + d, nz)

    def y_peer(d):
        return lax.rem(y_at + d, ny)

    def tp_peer(d):
        return lax.rem(tp + d, ntp)

    def remote(src, dst, send, recv, where):
        return pltpu.make_async_remote_copy(
            src_ref=src, dst_ref=dst, send_sem=send, recv_sem=recv, device_id=where, device_id_type=MESH
        )

    loads = [
        pltpu.make_async_copy(k_hbm, xin.at[1], load_sem.at[1]),
        pltpu.make_async_copy(v_hbm, xin.at[2], load_sem.at[2]),
        pltpu.make_async_copy(q_hbm, xin.at[0], load_sem.at[0]),
        pltpu.make_async_copy(go_hbm, go_v, load_sem.at[3]),
    ]
    for load in loads:
        load.start()

    barrier = pltpu.get_barrier_semaphore()
    partners = [(nxt, tp), (prv, tp)]
    partners += [(ctx, tp_peer(d)) for d in range(1, ntp)]
    partners += [(y_at * nz + z_peer(d), tp) for d in range(1, nz)]
    partners += [(y_peer(d) * nz + z_at, tp) for d in range(1, ny)]
    for where in partners:
        pl.semaphore_signal(barrier, inc=1, device_id=where, device_id_type=MESH)

    for a in range(3):
        taps = sw_ref[a].astype(F32)
        for c in range(nt):
            wsc[c, a, 0:SHORT, :] = taps[:, c * LANES : (c + 1) * LANES]
    gain_row = gain_ref[...].astype(F32)
    for c in range(nt):
        wsc[c, 3, 0:1, :] = gain_row[:, c * LANES : (c + 1) * LANES]
    filt32[...] = filt_ref[...].astype(F32)
    filt_rev[...] = jnp.dot(filt_ref[...], mirror().astype(BF16), preferred_element_type=F32)

    docs_f = docs_ref[...].astype(F32)
    own = [docs_f[0:1], docs_f[1:2]]
    own_col = [as_column(row) for row in own]
    for n in range(2):
        dcol[8 + HALF * n : 8 + HALF * (n + 1), :] = jnp.broadcast_to(own_col[n], (HALF, LANES))

    def short_masks(start, size):
        here = dcol[8 + start : 8 + start + size, :]
        m1[start : start + size, :] = (dcol[7 + start : 7 + start + size, :] == here).astype(F32)
        m2[start : start + size, :] = (dcol[6 + start : 6 + start + size, :] == here).astype(F32)

    short_masks(HALF, HALF)

    for load in loads[:3]:
        load.wait()
    for a in range(3):
        last = xin[a, ROWS - 16 : ROWS, :].astype(F32)
        edge_s[2 * a : 2 * a + 2, :] = last[14:16]
    edge_s[6:8, :] = jnp.zeros((2, channels), F32)

    pl.semaphore_wait(barrier, len(partners))

    doc_fwd = remote(docs_ref, docs_prev, doc_sem.at[0], doc_sem.at[1], (nxt, tp))
    doc_bwd = remote(docs_ref, docs_next, doc_sem.at[2], doc_sem.at[3], (prv, tp))
    edge = remote(edge_s, edge_r, edge_sem.at[0], edge_sem.at[1], (nxt, tp))
    doc_fwd.start()
    doc_bwd.start()
    edge.start()

    def cols(c):
        return pl.ds(pl.multiple_of(c * LANES, LANES), LANES)

    def feature(a, c, start):
        x0 = xf[a, c, pl.ds(8 + start, HALF), :]
        x1 = xf[a, c, pl.ds(7 + start, HALF), :]
        x2 = xf[a, c, pl.ds(6 + start, HALF), :]
        w = wsc[c, a]
        return (
            w[0:1] * x0
            + w[1:2] * x1 * m1[start : start + HALF, :]
            + w[2:3] * x2 * m2[start : start + HALF, :]
        )

    def halo1(c):
        return remote(
            prod.at[c, pl.ds(ROWS, HALF)], prod.at[c, pl.ds(0, HALF)], h1_send.at[c], h1_recv.at[c], (nxt, tp)
        )

    def halo2(c):
        return remote(
            gmix.at[c, pl.ds(0, HALF)], gmix.at[c, pl.ds(ROWS, HALF)], h2_send.at[c], h2_recv.at[c], (prv, tp)
        )

    def products(c, start):
        fk = feature(1, c, start)
        fv = feature(2, c, start)
        feats[1, c, start : start + HALF, :] = fk
        feats[2, c, start : start + HALF, :] = fv
        prod[c, HALF + start : 2 * HALF + start, :] = (fk * fv).astype(BF16)

    def late_half(c, carry):
        for a in (1, 2):
            xf[a, c, 8 : 8 + ROWS, :] = xin[a, :, cols(c)].astype(F32)
        products(c, HALF)
        halo1(c).start()
        return carry

    lax.fori_loop(0, nt, late_half, 0)

    doc_fwd.wait_recv()
    doc_bwd.wait_recv()
    edge.wait_recv()
    row_prev = jnp.where(ctx == 0, -1.0, docs_prev[1:2, :].astype(F32))
    row_next = jnp.where(ctx == n_ctx - 1, -1.0, docs_next[0:1, :].astype(F32))
    col_prev = as_column(row_prev)
    col_next = as_column(row_next)
    dcol[0:8, :] = jnp.broadcast_to(col_prev[HALF - 8 :], (8, LANES))
    dcol[8 + ROWS : 16 + ROWS, :] = jnp.broadcast_to(col_next[:8], (8, LANES))
    short_masks(0, HALF)
    short_masks(ROWS, 8)
    i_at, j_at = iota(0), iota(1)

    def pick(keep, column, row):
        return jnp.where(keep & (column == row), 1.0, 0.0)

    i_back = LANES - 1 - i_at
    back_col = [as_column(row, True) for row in own]
    before_rows = (row_prev, own[0])
    after_rows = (own[1], row_next)
    for n in range(2):
        fmask[n, :, 0:LANES] = pick(j_at > i_at, own_col[n], before_rows[n]).astype(BF16)
        fmask[n, :, LANES:] = pick(j_at <= i_at, own_col[n], own[n]).astype(BF16)
        fmask32[n, :, 0:LANES] = pick(j_at > i_back, back_col[n], before_rows[n])
        fmask32[n, :, LANES:] = pick(j_at <= i_back, back_col[n], own[n])
        bmask[n, :, 0:LANES] = pick(j_at >= i_at, own_col[n], own[n]).astype(BF16)
        bmask[n, :, LANES:] = pick(j_at < i_at, own_col[n], after_rows[n]).astype(BF16)

    def build(source, masks, target):
        def one(g, carry):
            c, at = lax.div(g, per_tile), lax.rem(g, per_tile)
            row = jnp.broadcast_to(source[pl.ds(g, 1), :], (HALF, LANES))
            band = pltpu.roll(row, 0, 1, stride=1, stride_axis=0).astype(BF16)
            rows = pl.ds(pl.multiple_of(at * HALF, HALF), HALF)
            for n in range(2):
                target[n, c, rows, 0:LANES] = band * masks[n, :, 0:LANES]
                target[n, c, rows, LANES:] = band * masks[n, :, LANES:]
            return carry

        lax.fori_loop(0, groups, one, 0)

    build(filt_rev, fmask, tf)

    def early_half(c, carry):
        xf[0, c, 8 : 8 + ROWS, :] = xin[0, :, cols(c)].astype(F32)
        for a in range(3):
            xf[a, c, 6:8, :] = edge_r[2 * a : 2 * a + 2, cols(c)]
        products(c, 0)
        for start in (0, HALF):
            feats[0, c, start : start + HALF, :] = feature(0, c, start)
        return carry

    lax.fori_loop(0, nt, early_half, 0)
    loads[3].wait()

    lane_group = lax.div(iota(1), width)

    def convolve(bands, window):
        small[...] = jnp.dot(bands, window, preferred_element_type=F32)
        value = small[0:HALF, :]
        for g in range(1, per_tile):
            value = jnp.where(lane_group == g, small[g * HALF : (g + 1) * HALF, :], value)
        return value

    acc[...] = jnp.zeros_like(acc)

    def forward(n):
        span = slice(n * HALF, (n + 1) * HALF)

        def one(c, carry):
            if n == 0:
                halo1(c).wait_recv()
            value = convolve(tf[n, c], prod[c, n * HALF : n * HALF + ROWS, :])
            mixed[c, span, :] = value
            y = feats[0, c, span, :] * value
            y_s[c, span, :] = y
            weighted = wsc[c, 3, 0:1, :] * go_v[span, cols(c)].astype(F32)
            acc[n, 0] += y * y
            acc[n, 1] += weighted * y
            return carry

        lax.fori_loop(0, nt, one, 0)

    forward(1)
    forward(0)

    stats[tp] = jnp.zeros((8, LANES), F32)
    for n in range(2):
        for kind in range(2):
            line = jnp.sum(acc[n, kind].T, axis=0, keepdims=True)
            stats[tp, 2 * kind + n : 2 * kind + n + 1, :] = line
    sends = [
        remote(stats.at[tp], stats.at[tp], st_send.at[d], st_recv.at[d], (ctx, tp_peer(d)))
        for d in range(1, ntp)
    ]
    for send in sends:
        send.start()
    build(filt32, bmask, tb)
    for d in range(1, ntp):
        came = stats.at[tp_peer(ntp - d)]
        remote(came, came, st_send.at[d], st_recv.at[d], (ctx, tp_peer(d))).wait_recv()
    sums = stats[0]
    for p in range(1, ntp):
        sums = sums + stats[p]
    scale = lax.rsqrt(sums[0:2] / total_channels + EPS)
    pull = scale * scale * scale * sums[2:4] / total_channels
    for n in range(2):
        scales[n, 0] = jnp.broadcast_to(as_column(scale[n : n + 1]), (HALF, LANES))
        scales[n, 1] = jnp.broadcast_to(as_column(pull[n : n + 1]), (HALF, LANES))

    def backward_norm(n):
        span = slice(n * HALF, (n + 1) * HALF)

        def one(c, carry):
            cot = go_v[span, cols(c)].astype(F32)
            y = y_s[c, span, :]
            row_scale = scales[n, 0]
            grad_y = row_scale * (wsc[c, 3, 0:1, :] * cot) - y * scales[n, 1]
            gain_part = jnp.sum(cot * y * row_scale, axis=0, keepdims=True)
            if n == 0:
                red[c, 17:18, :] = gain_part
            else:
                red[c, 17:18, :] += gain_part
            gmix[c, span, :] = (grad_y * feats[0, c, span, :]).astype(BF16)
            if n == 0:
                halo2(c).start()
            grads[0, c, span, :] = grad_y * mixed[c, span, :]
            if n == 0:
                tail_s[0:2, cols(c)] = grads[0, c, 0:2, :]
            return carry

        lax.fori_loop(0, nt, one, 0)

    backward_norm(0)
    backward_norm(1)

    def backward_conv(n):
        span = slice(n * HALF, (n + 1) * HALF)

        def one(c, carry):
            if n == 1:
                halo2(c).wait_recv()
            value = convolve(tb[n, c], gmix[c, n * HALF : n * HALF + ROWS, :])
            grads[1, c, span, :] = value * feats[2, c, span, :]
            grads[2, c, span, :] = value * feats[1, c, span, :]
            if n == 0:
                tail_s[2:4, cols(c)] = grads[1, c, 0:2, :]
                tail_s[4:6, cols(c)] = grads[2, c, 0:2, :]
            return carry

        lax.fori_loop(0, nt, one, 0)

    tail_s[6:8, :] = jnp.zeros((2, channels), F32)
    backward_conv(0)
    tail = remote(tail_s, tail_r, edge_sem.at[2], edge_sem.at[3], (prv, tp))
    tail.start()

    flip_s = flip().astype(BF16)

    def filter_sums(c, carry):
        for n in range(2):
            own_rows = jnp.dot(
                flip_s, gmix[c, n * HALF : (n + 1) * HALF, :], preferred_element_type=F32
            ).astype(BF16)
            for g in range(per_tile):
                keep = (lane_group == g).astype(BF16)
                lhs_s[g * HALF : (g + 1) * HALF, :] = own_rows * keep
            big[n] = lax.dot_general(
                lhs_s[...],
                prod[c, n * HALF : n * HALF + ROWS, :],
                (((1,), (1,)), ((), ())),
                preferred_element_type=F32,
            )
        lines = []
        for g in range(per_tile):
            rows = slice(g * HALF, (g + 1) * HALF)
            folded = jnp.zeros((HALF, LANES), F32)
            for n in range(2):
                folded += big[n, rows, 0:LANES] * fmask32[n, :, 0:LANES]
                folded += big[n, rows, LANES:] * fmask32[n, :, LANES:]
            turned = pltpu.roll(folded, 0, 1, stride=1, stride_axis=0)
            lines.append(jnp.sum(turned, axis=0, keepdims=True))
        lines = jnp.concatenate(lines, axis=0)
        red[c, 0:per_tile, :] = jnp.dot(
            lines, flip().astype(F32), preferred_element_type=F32, precision=lax.Precision.HIGHEST
        )
        return carry

    lax.fori_loop(0, nt, filter_sums, 0)
    backward_conv(1)
    tail.wait_recv()

    def finish(c, carry):
        for a in range(3):
            grads[a, c, ROWS : ROWS + 2, :] = tail_r[2 * a : 2 * a + 2, cols(c)]
            w = wsc[c, a]
            sums3 = [jnp.zeros((1, LANES), F32) for _ in range(SHORT)]
            for start in (0, HALF):
                x = xf[a, c, 8 + start : 8 + start + HALF, :]
                h0 = grads[a, c, start : start + HALF, :]
                h1 = grads[a, c, start + 1 : start + 1 + HALF, :] * m1[start + 1 : start + 1 + HALF, :]
                h2 = grads[a, c, start + 2 : start + 2 + HALF, :] * m2[start + 2 : start + 2 + HALF, :]
                value = w[0:1] * h0 + w[1:2] * h1 + w[2:3] * h2
                outs[a, start : start + HALF, cols(c)] = value.astype(BF16)
                for j, h in enumerate((h0, h1, h2)):
                    sums3[j] += jnp.sum(h * x, axis=0, keepdims=True)
            for j in range(SHORT):
                at = 8 + 3 * a + j
                red[c, at : at + 1, :] = sums3[j]
        red[c, 18:24, :] = jnp.zeros((6, LANES), F32)
        return carry

    lax.fori_loop(0, nt, finish, 0)
    stores = [
        pltpu.make_async_copy(outs.at[a], target, store_sem.at[a])
        for a, target in enumerate((gq_hbm, gk_hbm, gv_hbm))
    ]
    for store in stores:
        store.start()

    sends_a = [
        remote(red.at[z_peer(d)], red_a.at[d], ra_send.at[d], ra_recv.at[d], (y_at * nz + z_peer(d), tp))
        for d in range(1, nz)
    ]
    for send in sends_a:
        send.start()
    part = red[z_at]
    for d in range(1, nz):
        sends_a[d - 1].wait_recv()
        part = part + red_a[d]
    red_b[y_at] = part
    sends_b = [
        remote(red_b.at[y_at], red_b.at[y_at], rb_send.at[d], rb_recv.at[d], (y_peer(d) * nz + z_at, tp))
        for d in range(1, ny)
    ]
    for send in sends_b:
        send.start()
    for d in range(1, ny):
        came = red_b.at[y_peer(ny - d)]
        remote(came, came, rb_send.at[d], rb_recv.at[d], (y_peer(d) * nz + z_at, tp)).wait_recv()
    whole = red_b[0]
    for p in range(1, ny):
        whole = whole + red_b[p]
    fin[z_at] = whole * grad_scale
    sends_c = [
        remote(fin.at[z_at], fin.at[z_at], rc_send.at[d], rc_recv.at[d], (y_at * nz + z_peer(d), tp))
        for d in range(1, nz)
    ]
    for send in sends_c:
        send.start()
    for d in range(1, nz):
        came = fin.at[z_peer(nz - d)]
        remote(came, came, rc_send.at[d], rc_recv.at[d], (y_at * nz + z_peer(d), tp)).wait_recv()
    for c in range(nt):
        span = slice(c * LANES, (c + 1) * LANES)
        filt_out[c * per_tile : (c + 1) * per_tile, :] = fin[c, 0:per_tile, :]
        gain_out[:, span] = fin[c, 17:18, :]
        for a in range(3):
            short_out[a, :, span] = fin[c, 8 + 3 * a : 11 + 3 * a, :]

    for copy in [doc_fwd, doc_bwd, edge, tail] + sends + sends_a + sends_b + sends_c:
        copy.wait_send()

    def drain(c, carry):
        halo1(c).wait_send()
        halo2(c).wait_send()
        return carry

    lax.fori_loop(0, nt, drain, 0)
    for store in stores:
        store.wait()


def on_device(nz, q_in, k_in, v_in, grad_out, doc_ids, gain, filters, short_weight):
    rows, channels = q_in.shape
    groups, taps = filters.shape
    ntp = lax.axis_size("tp")
    ny = lax.axis_size("ctx") // nz
    nt = channels // LANES
    assert rows == ROWS and taps == HALF and nt == nz and groups == 8 * nt
    hbm = pl.BlockSpec(memory_space=pl.ANY)
    vmem = pl.BlockSpec(memory_space=pltpu.VMEM)
    tall = jax.ShapeDtypeStruct((rows, channels), BF16)
    dma = pltpu.SemaphoreType.DMA
    out = pl.pallas_call(
        functools.partial(kernel, ny, nz, ntp),
        name="mixer_backward",
        out_shape=(
            tall,
            tall,
            tall,
            jax.ShapeDtypeStruct((1, channels), F32),
            jax.ShapeDtypeStruct((groups, taps), F32),
            jax.ShapeDtypeStruct((3, SHORT, channels), F32),
        ),
        in_specs=[hbm] * 4 + [vmem] * 4,
        out_specs=(hbm, hbm, hbm, vmem, vmem, vmem),
        scratch_shapes=[
            pltpu.VMEM((3, rows, channels), BF16),
            pltpu.VMEM((rows, channels), BF16),
            pltpu.VMEM((3, nt, rows + 8, LANES), F32),
            pltpu.VMEM((3, nt, rows, LANES), F32),
            pltpu.VMEM((nt, rows, LANES), F32),
            pltpu.VMEM((nt, rows, LANES), F32),
            pltpu.VMEM((3, nt, rows + 8, LANES), F32),
            pltpu.VMEM((3, rows, channels), BF16),
            pltpu.VMEM((nt, rows + HALF, LANES), BF16),
            pltpu.VMEM((nt, rows + HALF, LANES), BF16),
            pltpu.VMEM((2, nt, 8 * HALF, 2 * LANES), BF16),
            pltpu.VMEM((2, nt, 8 * HALF, 2 * LANES), BF16),
            pltpu.VMEM((2, HALF, 2 * LANES), BF16),
            pltpu.VMEM((2, HALF, 2 * LANES), BF16),
            pltpu.VMEM((2, HALF, 2 * LANES), F32),
            pltpu.VMEM((groups, LANES), F32),
            pltpu.VMEM((groups, LANES), F32),
            pltpu.VMEM((nt, 4, 8, LANES), F32),
            pltpu.VMEM((rows + 16, LANES), F32),
            pltpu.VMEM((rows + 8, LANES), F32),
            pltpu.VMEM((rows + 8, LANES), F32),
            pltpu.VMEM((2, LANES), jnp.int32),
            pltpu.VMEM((2, LANES), jnp.int32),
            pltpu.VMEM((8, channels), F32),
            pltpu.VMEM((8, channels), F32),
            pltpu.VMEM((8, channels), F32),
            pltpu.VMEM((8, channels), F32),
            pltpu.VMEM((2, 2, HALF, LANES), F32),
            pltpu.VMEM((ntp, 8, LANES), F32),
            pltpu.VMEM((2, 2, HALF, LANES), F32),
            pltpu.VMEM((2, 8 * HALF, 2 * LANES), F32),
            pltpu.VMEM((8 * HALF, LANES), F32),
            pltpu.VMEM((8 * HALF, LANES), BF16),
            pltpu.VMEM((nt, CHUNK, LANES), F32),
            pltpu.VMEM((nz, CHUNK, LANES), F32),
            pltpu.VMEM((ny, CHUNK, LANES), F32),
            pltpu.VMEM((nz, CHUNK, LANES), F32),
            dma((4,)),
            dma((3,)),
            dma((4,)),
            dma((4,)),
            dma((nt,)),
            dma((nt,)),
            dma((nt,)),
            dma((nt,)),
            dma((ntp,)),
            dma((ntp,)),
            dma((nz,)),
            dma((nz,)),
            dma((ny,)),
            dma((ny,)),
            dma((nz,)),
            dma((nz,)),
        ],
        compiler_params=pltpu.CompilerParams(
            collective_id=0, has_side_effects=True, vmem_limit_bytes=60 * 1024 * 1024
        ),
    )(
        q_in,
        k_in,
        v_in,
        grad_out,
        doc_ids.reshape(2, LANES),
        gain.reshape(1, channels),
        filters,
        short_weight,
    )
    return out[0], out[1], out[2], out[3].reshape(channels), out[4], out[5]


def solution(mesh, ring=RING):
    return jax.shard_map(
        functools.partial(on_device, ring),
        mesh=mesh,
        in_specs=(
            P("ctx", "tp"),
            P("ctx", "tp"),
            P("ctx", "tp"),
            P("ctx", "tp"),
            P("ctx"),
            P("tp"),
            P("tp", None),
            P(None, None, "tp"),
        ),
        out_specs=(
            P("ctx", "tp"),
            P("ctx", "tp"),
            P("ctx", "tp"),
            P("tp"),
            P("tp", None),
            P(None, None, "tp"),
        ),
        check_vma=False,
    )
```

time: 357 us -> 70.7 us (0.20)
  waiting for transfers between devices: 143 us -> 0 us
  local copies, waits for them, and re-layouts: 96.4 us -> 7.07 us
  Pallas kernels: 0 us -> 62 us
  other arithmetic: 29.8 us -> 0 us
  matrix products: 24.4 us -> 0 us
  blocking collectives: 23.1 us -> 0 us
  starting transfers between devices: 21 us -> 0 us
  between operations: 15.1 us -> 0.66 us
    psum x1 -> x0, waiting for transfers between devices: 137 us -> none  [on_device(): grad_gain = lax.psum(gain_term, 'ctx')]
    pallas_call x0 -> x1, Pallas kernels: none -> 62 us  [on_device(): pl.pallas_call(functools.partial(kernel, ny, nz, ntp), name='mixer_backwa...]
    reshape x8 -> x1, local copies, waits for them, and re-layouts: 53.7 us -> 1.28 us  [on_device(): gain.reshape(1, channels)]
    dot_general x6 -> x0, matrix products: 24.4 us -> none  [the longest x2 11 us: on_device(): jnp.einsum('igc,jgc->gij', own_block, behind, preferred_element_type=jnp....]
    psum x2 -> x0, blocking collectives: 23.1 us -> none  [on_device(): lax.psum((jnp.sum(y_out * y_out, axis=1), jnp.sum(weighted * y_out, axis=...]
    ppermute x7 -> x0, starting transfers between devices: 21 us -> none  [shifted(): return lax.ppermute(value, axis, pairs)]
    slice x20 -> x0, local copies, waits for them, and re-layouts: 16.1 us -> none  [the longest x2 4.52 us: banded(): repeated = jnp.tile(padded, (1, block_rows))[:, :block_rows * span_cols]]
    convert_element_type x9 -> x0, other arithmetic: 15.3 us -> none  [the longest x2 5.21 us: unfeature(): return running.astype(jnp.bfloat16)]
  transfers between devices with their start and end apart: 8 -> 0, of which waited for: 2 -> 0; matrix products, arithmetic and copies ran while one was open for 33% -> 0% of each run, Pallas kernels for 0% -> 0%
where the time goes in v1:
time: 70.7 us; the launch traced here: 69.7 us
  Pallas kernels  62 us (88%)
  local copies, waits for them, and re-layouts  7.07 us (10%)
    pallas_call x1, Pallas kernels, on_device(): pl.pallas_call(functools.partial(kernel, ny, nz, ntp), name='mixer_backwa...  62 us
    unnamed x16, local copies, waits for them, and re-layouts  5.79 us

profile of v1, /device:TPU:2, one launch (start us, length us, event | category | flops | bytes accessed | tf_op | source)
XLA Modules:
  0.0 69.7 jit_solution(17237158350307493766)
XLA Ops:
  0.6 1.3 %reshape.22.gain_ref = bf16[1,1024]{1,0:T(2,128)(2,1)} reshape(bf16[1024]{0:T(1024)(128)(2,1)} %param.13) | data formatting | bytes 4096 | tf_op jit(solution)/shard_map/reshape | solution.py:600
  1.9 62.0 %mixer_backward.1 = (bf16[256,1024]{1,0:T(8,128)(2,1)}, bf16[256,1024]{1,0:T(8,128)(2,1)}, bf16[256,1024]{1,0:T(8,128)(2,1)}, f32[1,1024]{1,0:T(1,128)}, f32[64,128]{1,0:T(8,128)}, /*index=5*/f32[3,3,1024]{2,1,0:T(4,128)}) custom-call(bf16[256,1024]{1,0:T(8,128)(2,1)} %q_hbm.1, bf16[256,1024]{1,0:T(8,128)(2,1)} %k_hbm.1, bf16[256,1024]{1,0:T(8,128)(2,1)} %v_hbm.1, ...), custom_call_target="tpu_custom_call" | custom-call | tf_op jit(solution)/shard_map/mixer_backward/pallas_call | solution.py:523
  63.9 0.0 copy-start.1
  63.9 1.9 %copy.20 = bf16[256,1024]{1,0:T(8,128)(2,1)} copy(bf16[256,1024]{1,0:T(8,128)(2,1)} %get-tuple-element.24) | data formatting | bytes 1048576
  65.8 0.0 copy-done.1
  65.8 0.0 copy-start
  65.8 0.8 %copy.21 = bf16[256,1024]{1,0:T(8,128)(2,1)} copy(bf16[256,1024]{1,0:T(8,128)(2,1)S(1)} %copy-done.1) | data formatting | bytes 1048576
  66.6 0.4 copy-done
  67.0 0.0 copy-start.4
  67.1 0.0 copy-start.3
  67.1 0.8 %copy.22 = bf16[256,1024]{1,0:T(8,128)(2,1)} copy(bf16[256,1024]{1,0:T(8,128)(2,1)S(1)} %copy-done) | data formatting | bytes 1048576
  67.8 0.0 copy-done.4
  67.8 0.0 copy-start.2
  67.9 0.6 copy.23
  68.4 0.0 copy-done.3
  68.4 0.6 copy.24
  69.1 0.0 copy-done.2
  69.1 0.6 copy.25
Async XLA Ops:
  63.9 1.9 %copy-start.1 = (bf16[256,1024]{1,0:T(8,128)(2,1)S(1)}, bf16[256,1024]{1,0:T(8,128)(2,1)}, u32[]{:S(2)}) copy-start(bf16[256,1024]{1,0:T(8,128)(2,1)} %get-tuple-element.25) | copy-start | bytes 1572868
  65.8 1.2 %copy-start = (bf16[256,1024]{1,0:T(8,128)(2,1)S(1)}, bf16[256,1024]{1,0:T(8,128)(2,1)}, u32[]{:S(2)}) copy-start(bf16[256,1024]{1,0:T(8,128)(2,1)} %get-tuple-element.26) | copy-start | bytes 1572868
  67.0 0.8 %copy-start.4 = (f32[1,1024]{1,0:T(1,128)S(1)}, f32[1,1024]{1,0:T(1,128)}, u32[]{:S(2)}) copy-start(f32[1,1024]{1,0:T(1,128)} %get-tuple-element.15) | copy-start | bytes 12292
  67.1 1.4 %copy-start.3 = (f32[64,128]{1,0:T(8,128)S(1)}, f32[64,128]{1,0:T(8,128)}, u32[]{:S(2)}) copy-start(f32[64,128]{1,0:T(8,128)} %get-tuple-element.28) | copy-start | bytes 98308
  67.8 1.2 %copy-start.2 = (f32[3,3,1024]{2,1,0:T(4,128)S(1)}, f32[3,3,1024]{2,1,0:T(4,128)}, u32[]{:S(2)}) copy-start(f32[3,3,1024]{2,1,0:T(4,128)} %get-tuple-element.29) | copy-start | bytes 110596

commit v2 on v1

--- a/solution.py
+++ b/solution.py
@@ -24,8 +24,8 @@
     return lax.broadcasted_iota(jnp.int32, (LANES, LANES), axis)
 
 
-def as_column(row, flipped=False):
-    eye = flip() if flipped else iota(0) == iota(1)
+def as_column(row):
+    eye = iota(0) == iota(1)
     spread = jnp.where(eye, jnp.broadcast_to(row, (LANES, LANES)), 0.0)
     return jnp.sum(spread, axis=1, keepdims=True)
 
@@ -51,9 +51,9 @@
     gain_ref,
     filt_ref,
     sw_ref,
-    gq_hbm,
-    gk_hbm,
-    gv_hbm,
+    gq_ref,
+    gk_ref,
+    gv_ref,
     gain_out,
     filt_out,
     short_out,
@@ -64,11 +64,10 @@
     mixed,
     y_s,
     grads,
-    outs,
     prod,
     gmix,
-    tf,
-    tb,
+    ring_f,
+    ring_b,
     fmask,
     bmask,
     fmask32,
@@ -90,12 +89,12 @@
     big,
     small,
     lhs_s,
+    turned_s,
     red,
     red_a,
     red_b,
     fin,
     load_sem,
-    store_sem,
     doc_sem,
     edge_sem,
     h1_send,
@@ -112,6 +111,7 @@
     rc_recv,
 ):
     nt = nz
+    outs = (gq_ref, gk_ref, gv_ref)
     groups = filt_ref.shape[0]
     per_tile = groups // nt
     width = LANES // per_tile
@@ -161,9 +161,8 @@
         taps = sw_ref[a].astype(F32)
         for c in range(nt):
             wsc[c, a, 0:SHORT, :] = taps[:, c * LANES : (c + 1) * LANES]
-    gain_row = gain_ref[...].astype(F32)
     for c in range(nt):
-        wsc[c, 3, 0:1, :] = gain_row[:, c * LANES : (c + 1) * LANES]
+        wsc[c, 3, 0:1, :] = gain_ref[c * LANES : (c + 1) * LANES].astype(F32).reshape(1, LANES)
     filt32[...] = filt_ref[...].astype(F32)
     filt_rev[...] = jnp.dot(filt_ref[...], mirror().astype(BF16), preferred_element_type=F32)
 
@@ -235,6 +234,19 @@
         return carry
 
     lax.fori_loop(0, nt, late_half, 0)
+
+    def build(source, target):
+        def one(c, carry):
+            rows = source[pl.ds(pl.multiple_of(c * per_tile, per_tile), per_tile), :]
+            for g in range(per_tile):
+                row = jnp.broadcast_to(rows[g : g + 1], (HALF, LANES))
+                band = pltpu.roll(row, 0, 1, stride=1, stride_axis=0)
+                target[c, g * HALF : (g + 1) * HALF, :] = band.astype(BF16)
+            return carry
+
+        lax.fori_loop(0, nt, one, 0)
+
+    build(filt_rev, ring_f)
 
     doc_fwd.wait_recv()
     doc_bwd.wait_recv()
@@ -252,32 +264,16 @@
     def pick(keep, column, row):
         return jnp.where(keep & (column == row), 1.0, 0.0)
 
-    i_back = LANES - 1 - i_at
-    back_col = [as_column(row, True) for row in own]
+    flip_s = flip().astype(BF16)
     before_rows = (row_prev, own[0])
     after_rows = (own[1], row_next)
     for n in range(2):
-        fmask[n, :, 0:LANES] = pick(j_at > i_at, own_col[n], before_rows[n]).astype(BF16)
-        fmask[n, :, LANES:] = pick(j_at <= i_at, own_col[n], own[n]).astype(BF16)
-        fmask32[n, :, 0:LANES] = pick(j_at > i_back, back_col[n], before_rows[n])
-        fmask32[n, :, LANES:] = pick(j_at <= i_back, back_col[n], own[n])
-        bmask[n, :, 0:LANES] = pick(j_at >= i_at, own_col[n], own[n]).astype(BF16)
-        bmask[n, :, LANES:] = pick(j_at < i_at, own_col[n], after_rows[n]).astype(BF16)
-
-    def build(source, masks, target):
-        def one(g, carry):
-            c, at = lax.div(g, per_tile), lax.rem(g, per_tile)
-            row = jnp.broadcast_to(source[pl.ds(g, 1), :], (HALF, LANES))
-            band = pltpu.roll(row, 0, 1, stride=1, stride_axis=0).astype(BF16)
-            rows = pl.ds(pl.multiple_of(at * HALF, HALF), HALF)
-            for n in range(2):
-                target[n, c, rows, 0:LANES] = band * masks[n, :, 0:LANES]
-                target[n, c, rows, LANES:] = band * masks[n, :, LANES:]
-            return carry
-
-        lax.fori_loop(0, groups, one, 0)
-
-    build(filt_rev, fmask, tf)
+        fmask[n, 0] = pick(j_at > i_at, own_col[n], before_rows[n]).astype(BF16)
+        fmask[n, 1] = pick(j_at <= i_at, own_col[n], own[n]).astype(BF16)
+        for side in range(2):
+            fmask32[n, side] = jnp.dot(fmask[n, side], flip_s, preferred_element_type=F32)
+        bmask[n, 0] = pick(j_at >= i_at, own_col[n], own[n]).astype(BF16)
+        bmask[n, 1] = pick(j_at < i_at, own_col[n], after_rows[n]).astype(BF16)
 
     def early_half(c, carry):
         xf[0, c, 8 : 8 + ROWS, :] = xin[0, :, cols(c)].astype(F32)
@@ -293,31 +289,45 @@
 
     lane_group = lax.div(iota(1), width)
 
-    def convolve(bands, window):
-        small[...] = jnp.dot(bands, window, preferred_element_type=F32)
-        value = small[0:HALF, :]
+    def convolve(bands, masks, window, slot):
+        for g in range(per_tile):
+            rows = slice(g * HALF, (g + 1) * HALF)
+            band = bands[rows, :]
+            for side in range(2):
+                lhs_s[slot, side, rows, :] = band * masks[side]
+        lhs = jnp.concatenate([lhs_s[slot, 0], lhs_s[slot, 1]], axis=1)
+        small[slot] = jnp.dot(lhs, window, preferred_element_type=F32)
+        value = small[slot, 0:HALF, :]
         for g in range(1, per_tile):
-            value = jnp.where(lane_group == g, small[g * HALF : (g + 1) * HALF, :], value)
+            value = jnp.where(lane_group == g, small[slot, g * HALF : (g + 1) * HALF, :], value)
         return value
+
+    def tiles(body, ready=None, unroll=2):
+        def step(i, carry):
+            if ready is not None:
+                for u in range(unroll):
+                    ready(i * unroll + u)
+            for u in range(unroll):
+                body(i * unroll + u, u)
+            return carry
+
+        lax.fori_loop(0, nt // unroll, step, 0)
 
     acc[...] = jnp.zeros_like(acc)
 
     def forward(n):
         span = slice(n * HALF, (n + 1) * HALF)
 
-        def one(c, carry):
-            if n == 0:
-                halo1(c).wait_recv()
-            value = convolve(tf[n, c], prod[c, n * HALF : n * HALF + ROWS, :])
+        def one(c, slot):
+            value = convolve(ring_f.at[c], fmask[n], prod[c, n * HALF : n * HALF + ROWS, :], slot)
             mixed[c, span, :] = value
             y = feats[0, c, span, :] * value
             y_s[c, span, :] = y
             weighted = wsc[c, 3, 0:1, :] * go_v[span, cols(c)].astype(F32)
             acc[n, 0] += y * y
             acc[n, 1] += weighted * y
-            return carry
-
-        lax.fori_loop(0, nt, one, 0)
+
+        tiles(one, (lambda c: halo1(c).wait_recv()) if n == 0 else None)
 
     forward(1)
     forward(0)
@@ -333,7 +343,7 @@
     ]
     for send in sends:
         send.start()
-    build(filt32, bmask, tb)
+    build(filt32, ring_b)
     for d in range(1, ntp):
         came = stats.at[tp_peer(ntp - d)]
         remote(came, came, st_send.at[d], st_recv.at[d], (ctx, tp_peer(d))).wait_recv()
@@ -375,53 +385,42 @@
     def backward_conv(n):
         span = slice(n * HALF, (n + 1) * HALF)
 
-        def one(c, carry):
-            if n == 1:
-                halo2(c).wait_recv()
-            value = convolve(tb[n, c], gmix[c, n * HALF : n * HALF + ROWS, :])
+        def one(c, slot):
+            value = convolve(ring_b.at[c], bmask[n], gmix[c, n * HALF : n * HALF + ROWS, :], slot)
             grads[1, c, span, :] = value * feats[2, c, span, :]
             grads[2, c, span, :] = value * feats[1, c, span, :]
             if n == 0:
                 tail_s[2:4, cols(c)] = grads[1, c, 0:2, :]
                 tail_s[4:6, cols(c)] = grads[2, c, 0:2, :]
-            return carry
-
-        lax.fori_loop(0, nt, one, 0)
+
+        tiles(one, (lambda c: halo2(c).wait_recv()) if n == 1 else None)
 
     tail_s[6:8, :] = jnp.zeros((2, channels), F32)
     backward_conv(0)
     tail = remote(tail_s, tail_r, edge_sem.at[2], edge_sem.at[3], (prv, tp))
     tail.start()
 
-    flip_s = flip().astype(BF16)
-
     def filter_sums(c, carry):
+        for at in range(3):
+            block = prod[c, at * HALF : (at + 1) * HALF, :]
+            turned_s[at] = jnp.dot(flip_s, block, preferred_element_type=F32).astype(BF16)
         for n in range(2):
-            own_rows = jnp.dot(
-                flip_s, gmix[c, n * HALF : (n + 1) * HALF, :], preferred_element_type=F32
-            ).astype(BF16)
+            own_rows = gmix[c, n * HALF : (n + 1) * HALF, :]
             for g in range(per_tile):
                 keep = (lane_group == g).astype(BF16)
-                lhs_s[g * HALF : (g + 1) * HALF, :] = own_rows * keep
+                lhs_s[n, 0, g * HALF : (g + 1) * HALF, :] = own_rows * keep
+            window = jnp.concatenate([turned_s[n], turned_s[n + 1]], axis=0)
             big[n] = lax.dot_general(
-                lhs_s[...],
-                prod[c, n * HALF : n * HALF + ROWS, :],
-                (((1,), (1,)), ((), ())),
-                preferred_element_type=F32,
+                lhs_s[n, 0], window, (((1,), (1,)), ((), ())), preferred_element_type=F32
             )
-        lines = []
         for g in range(per_tile):
             rows = slice(g * HALF, (g + 1) * HALF)
             folded = jnp.zeros((HALF, LANES), F32)
             for n in range(2):
-                folded += big[n, rows, 0:LANES] * fmask32[n, :, 0:LANES]
-                folded += big[n, rows, LANES:] * fmask32[n, :, LANES:]
-            turned = pltpu.roll(folded, 0, 1, stride=1, stride_axis=0)
-            lines.append(jnp.sum(turned, axis=0, keepdims=True))
-        lines = jnp.concatenate(lines, axis=0)
-        red[c, 0:per_tile, :] = jnp.dot(
-            lines, flip().astype(F32), preferred_element_type=F32, precision=lax.Precision.HIGHEST
-        )
+                folded += big[n, rows, 0:LANES] * fmask32[n, 0]
+                folded += big[n, rows, LANES:] * fmask32[n, 1]
+            turned = pltpu.roll(folded, 1, 1, stride=1, stride_axis=0)
+            red[c, g : g + 1, :] = jnp.sum(turned, axis=0, keepdims=True)
         return carry
 
     lax.fori_loop(0, nt, filter_sums, 0)
@@ -439,7 +438,7 @@
                 h1 = grads[a, c, start + 1 : start + 1 + HALF, :] * m1[start + 1 : start + 1 + HALF, :]
                 h2 = grads[a, c, start + 2 : start + 2 + HALF, :] * m2[start + 2 : start + 2 + HALF, :]
                 value = w[0:1] * h0 + w[1:2] * h1 + w[2:3] * h2
-                outs[a, start : start + HALF, cols(c)] = value.astype(BF16)
+                outs[a][start : start + HALF, cols(c)] = value.astype(BF16)
                 for j, h in enumerate((h0, h1, h2)):
                     sums3[j] += jnp.sum(h * x, axis=0, keepdims=True)
             for j in range(SHORT):
@@ -449,13 +448,6 @@
         return carry
 
     lax.fori_loop(0, nt, finish, 0)
-    stores = [
-        pltpu.make_async_copy(outs.at[a], target, store_sem.at[a])
-        for a, target in enumerate((gq_hbm, gk_hbm, gv_hbm))
-    ]
-    for store in stores:
-        store.start()
-
     sends_a = [
         remote(red.at[z_peer(d)], red_a.at[d], ra_send.at[d], ra_recv.at[d], (y_at * nz + z_peer(d), tp))
         for d in range(1, nz)
@@ -505,8 +497,24 @@
         return carry
 
     lax.fori_loop(0, nt, drain, 0)
-    for store in stores:
-        store.wait()
+
+
+def resident(shape, dtype):
+    return pltpu.VMEM(shape, dtype)
+
+
+def pinned(value):
+    return pltpu.with_memory_space_constraint(value, pltpu.VMEM)
+
+
+def publish(*refs):
+    count = (len(refs) - 1) // 2
+    sem = refs[-1]
+    copies = [pltpu.make_async_copy(refs[i], refs[count + i], sem.at[i]) for i in range(count)]
+    for copy in copies:
+        copy.start()
+    for copy in copies:
+        copy.wait()
 
 
 def on_device(nz, q_in, k_in, v_in, grad_out, doc_ids, gain, filters, short_weight):
@@ -518,21 +526,21 @@
     assert rows == ROWS and taps == HALF and nt == nz and groups == 8 * nt
     hbm = pl.BlockSpec(memory_space=pl.ANY)
     vmem = pl.BlockSpec(memory_space=pltpu.VMEM)
-    tall = jax.ShapeDtypeStruct((rows, channels), BF16)
+    tall = resident((rows, channels), BF16)
     dma = pltpu.SemaphoreType.DMA
-    out = pl.pallas_call(
+    held = pl.pallas_call(
         functools.partial(kernel, ny, nz, ntp),
         name="mixer_backward",
         out_shape=(
             tall,
             tall,
             tall,
-            jax.ShapeDtypeStruct((1, channels), F32),
-            jax.ShapeDtypeStruct((groups, taps), F32),
-            jax.ShapeDtypeStruct((3, SHORT, channels), F32),
+            resident((1, channels), F32),
+            resident((groups, taps), F32),
+            resident((3, SHORT, channels), F32),
         ),
-        in_specs=[hbm] * 4 + [vmem] * 4,
-        out_specs=(hbm, hbm, hbm, vmem, vmem, vmem),
+        in_specs=[pl.BlockSpec(memory_space=pltpu.HBM)] * 4 + [vmem] * 4,
+        out_specs=(vmem,) * 6,
         scratch_shapes=[
             pltpu.VMEM((3, rows, channels), BF16),
             pltpu.VMEM((rows, channels), BF16),
@@ -541,14 +549,13 @@
             pltpu.VMEM((nt, rows, LANES), F32),
             pltpu.VMEM((nt, rows, LANES), F32),
             pltpu.VMEM((3, nt, rows + 8, LANES), F32),
-            pltpu.VMEM((3, rows, channels), BF16),
             pltpu.VMEM((nt, rows + HALF, LANES), BF16),
             pltpu.VMEM((nt, rows + HALF, LANES), BF16),
-            pltpu.VMEM((2, nt, 8 * HALF, 2 * LANES), BF16),
-            pltpu.VMEM((2, nt, 8 * HALF, 2 * LANES), BF16),
-            pltpu.VMEM((2, HALF, 2 * LANES), BF16),
-            pltpu.VMEM((2, HALF, 2 * LANES), BF16),
-            pltpu.VMEM((2, HALF, 2 * LANES), F32),
+            pltpu.VMEM((nt, 8 * HALF, LANES), BF16),
+            pltpu.VMEM((nt, 8 * HALF, LANES), BF16),
+            pltpu.VMEM((2, 2, HALF, LANES), BF16),
+            pltpu.VMEM((2, 2, HALF, LANES), BF16),
+            pltpu.VMEM((2, 2, HALF, LANES), F32),
             pltpu.VMEM((groups, LANES), F32),
             pltpu.VMEM((groups, LANES), F32),
             pltpu.VMEM((nt, 4, 8, LANES), F32),
@@ -565,14 +572,14 @@
             pltpu.VMEM((ntp, 8, LANES), F32),
             pltpu.VMEM((2, 2, HALF, LANES), F32),
             pltpu.VMEM((2, 8 * HALF, 2 * LANES), F32),
-            pltpu.VMEM((8 * HALF, LANES), F32),
-            pltpu.VMEM((8 * HALF, LANES), BF16),
+            pltpu.VMEM((2, 8 * HALF, LANES), F32),
+            pltpu.VMEM((2, 2, 8 * HALF, LANES), BF16),
+            pltpu.VMEM((3, HALF, LANES), BF16),
             pltpu.VMEM((nt, CHUNK, LANES), F32),
             pltpu.VMEM((nz, CHUNK, LANES), F32),
             pltpu.VMEM((ny, CHUNK, LANES), F32),
             pltpu.VMEM((nz, CHUNK, LANES), F32),
             dma((4,)),
-            dma((3,)),
             dma((4,)),
             dma((4,)),
             dma((nt,)),
@@ -597,10 +604,18 @@
         v_in,
         grad_out,
         doc_ids.reshape(2, LANES),
-        gain.reshape(1, channels),
+        gain,
         filters,
         short_weight,
     )
+    out = pl.pallas_call(
+        publish,
+        name="publish",
+        out_shape=[jax.ShapeDtypeStruct(x.shape, x.dtype) for x in held],
+        in_specs=[vmem] * 6,
+        out_specs=[hbm] * 6,
+        scratch_shapes=[dma((6,))],
+    )(*[pinned(x) for x in held])
     return out[0], out[1], out[2], out[3].reshape(channels), out[4], out[5]
 
 

time: 70.7 us -> 52.1 us (0.74)
  the two profiles are of different devices: /device:TPU:2 before, /device:TPU:16 now
where the time goes in v2:
time: 52.1 us; the launch traced here: 52 us
  Pallas kernels  51.3 us (98%)
  between operations  0.64 us (1%)
    pallas_call x1, Pallas kernels, on_device(): pl.pallas_call(functools.partial(kernel, ny, nz, ntp), name='mixer_backwa...  50.1 us
    pallas_call x1, Pallas kernels, on_device(): pl.pallas_call(publish, name='publish', out_shape=[jax.ShapeDtypeStruct(x...  1.21 us

profile of v2, /device:TPU:16, one launch (start us, length us, event | category | flops | bytes accessed | tf_op | source)
XLA Modules:
  0.0 52.0 jit_solution(12228902302075533181)
XLA Ops:
  0.6 50.1 %mixer_backward.1 = (bf16[256,1024]{1,0:T(8,128)(2,1)S(1)}, bf16[256,1024]{1,0:T(8,128)(2,1)S(1)}, bf16[256,1024]{1,0:T(8,128)(2,1)S(1)}, f32[1,1024]{1,0:T(1,12...) custom-call(bf16[256,1024]{1,0:T(8,128)(2,1)} %q_hbm.1, bf16[256,1024]{1,0:T(8,128)(2,1)} %k_hbm.1, ...), custom_call_target="tpu_custom_call" | custom-call | tf_op jit(solution)/shard_map/mixer_backward/pallas_call | solution.py:531
  50.8 1.2 %publish.1 = (bf16[256,1024]{1,0:T(8,128)(2,1)}, bf16[256,1024]{1,0:T(8,128)(2,1)}, bf16[256,1024]{1,0:T(8,128)(2,1)}, f32[1,1024]{1,0:T(1,128)}, f32[64,128]{1,0:T(8,128)}, /*index=5*/f32[3,3,1024]{2,1,0:T(4,128)}) custom-call(bf16[256,1024]{1,0:T(8,128)(2,1)S(1)} %get-tuple-element.18.refs_0_, bf16[256,1024]{1,0:T(8,128)(2,1)S(1)} %get-tuple-element.19.refs_1_, ...), custom_call_target="tpu_custom_call" | custom-call | tf_op jit(solution)/shard_map/publish/pallas_call | solution.py:611

commit v3 on v2

--- a/solution.py
+++ b/solution.py
@@ -17,7 +17,7 @@
 SHORT = 3
 EPS = 1e-06
 RING = 8
-CHUNK = 24
+SPLIT = 120
 
 
 def iota(axis):
@@ -83,17 +83,23 @@
     edge_r,
     tail_s,
     tail_r,
+    tail_q_s,
+    tail_q_r,
     acc,
     stats,
     scales,
     big,
     small,
     lhs_s,
-    turned_s,
-    red,
-    red_a,
-    red_b,
-    fin,
+    mirrored,
+    red_e,
+    red_l,
+    e1,
+    e2,
+    fin_e,
+    l1,
+    l2,
+    fin_l,
     load_sem,
     doc_sem,
     edge_sem,
@@ -103,12 +109,19 @@
     h2_recv,
     st_send,
     st_recv,
-    ra_send,
-    ra_recv,
-    rb_send,
-    rb_recv,
-    rc_send,
-    rc_recv,
+    tq_sem,
+    e1_send,
+    e1_recv,
+    e2_send,
+    e2_recv,
+    e3_send,
+    e3_recv,
+    l1_send,
+    l1_recv,
+    l2_send,
+    l2_recv,
+    l3_send,
+    l3_recv,
 ):
     nt = nz
     outs = (gq_ref, gk_ref, gv_ref)
@@ -186,14 +199,9 @@
         edge_s[2 * a : 2 * a + 2, :] = last[14:16]
     edge_s[6:8, :] = jnp.zeros((2, channels), F32)
 
-    pl.semaphore_wait(barrier, len(partners))
-
     doc_fwd = remote(docs_ref, docs_prev, doc_sem.at[0], doc_sem.at[1], (nxt, tp))
     doc_bwd = remote(docs_ref, docs_next, doc_sem.at[2], doc_sem.at[3], (prv, tp))
     edge = remote(edge_s, edge_r, edge_sem.at[0], edge_sem.at[1], (nxt, tp))
-    doc_fwd.start()
-    doc_bwd.start()
-    edge.start()
 
     def cols(c):
         return pl.ds(pl.multiple_of(c * LANES, LANES), LANES)
@@ -230,10 +238,19 @@
         for a in (1, 2):
             xf[a, c, 8 : 8 + ROWS, :] = xin[a, :, cols(c)].astype(F32)
         products(c, HALF)
+        return carry
+
+    lax.fori_loop(0, nt, late_half, 0)
+    pl.semaphore_wait(barrier, len(partners))
+    doc_fwd.start()
+    doc_bwd.start()
+    edge.start()
+
+    def send_product(c, carry):
         halo1(c).start()
         return carry
 
-    lax.fori_loop(0, nt, late_half, 0)
+    lax.fori_loop(0, nt, send_product, 0)
 
     def build(source, target):
         def one(c, carry):
@@ -247,6 +264,7 @@
         lax.fori_loop(0, nt, one, 0)
 
     build(filt_rev, ring_f)
+    build(filt32, ring_b)
 
     doc_fwd.wait_recv()
     doc_bwd.wait_recv()
@@ -315,6 +333,14 @@
 
     acc[...] = jnp.zeros_like(acc)
 
+    def mirror_products(c, carry):
+        for at in range(3):
+            block = prod[c, at * HALF : (at + 1) * HALF, :]
+            mirrored[c, at * HALF : (at + 1) * HALF, :] = jnp.dot(
+                flip_s, block, preferred_element_type=F32
+            ).astype(BF16)
+        return carry
+
     def forward(n):
         span = slice(n * HALF, (n + 1) * HALF)
 
@@ -343,7 +369,7 @@
     ]
     for send in sends:
         send.start()
-    build(filt32, ring_b)
+    lax.fori_loop(0, nt, mirror_products, 0)
     for d in range(1, ntp):
         came = stats.at[tp_peer(ntp - d)]
         remote(came, came, st_send.at[d], st_recv.at[d], (ctx, tp_peer(d))).wait_recv()
@@ -366,20 +392,23 @@
             grad_y = row_scale * (wsc[c, 3, 0:1, :] * cot) - y * scales[n, 1]
             gain_part = jnp.sum(cot * y * row_scale, axis=0, keepdims=True)
             if n == 0:
-                red[c, 17:18, :] = gain_part
+                red_e[c, 8:9, :] = gain_part
             else:
-                red[c, 17:18, :] += gain_part
+                red_e[c, 8:9, :] += gain_part
             gmix[c, span, :] = (grad_y * feats[0, c, span, :]).astype(BF16)
             if n == 0:
                 halo2(c).start()
             grads[0, c, span, :] = grad_y * mixed[c, span, :]
             if n == 0:
-                tail_s[0:2, cols(c)] = grads[0, c, 0:2, :]
+                tail_q_s[0:2, cols(c)] = grads[0, c, 0:2, :]
             return carry
 
         lax.fori_loop(0, nt, one, 0)
 
+    tail_q_s[2:8, :] = jnp.zeros((6, channels), F32)
     backward_norm(0)
+    tail_q = remote(tail_q_s, tail_q_r, tq_sem.at[0], tq_sem.at[1], (prv, tp))
+    tail_q.start()
     backward_norm(1)
 
     def backward_conv(n):
@@ -392,103 +421,152 @@
             if n == 0:
                 tail_s[2:4, cols(c)] = grads[1, c, 0:2, :]
                 tail_s[4:6, cols(c)] = grads[2, c, 0:2, :]
+            else:
+                finish_last(c)
 
         tiles(one, (lambda c: halo2(c).wait_recv()) if n == 1 else None)
 
+    tail_s[0:2, :] = jnp.zeros((2, channels), F32)
     tail_s[6:8, :] = jnp.zeros((2, channels), F32)
     backward_conv(0)
     tail = remote(tail_s, tail_r, edge_sem.at[2], edge_sem.at[3], (prv, tp))
     tail.start()
 
-    def filter_sums(c, carry):
-        for at in range(3):
-            block = prod[c, at * HALF : (at + 1) * HALF, :]
-            turned_s[at] = jnp.dot(flip_s, block, preferred_element_type=F32).astype(BF16)
+    def filter_sums(c, slot):
         for n in range(2):
             own_rows = gmix[c, n * HALF : (n + 1) * HALF, :]
             for g in range(per_tile):
                 keep = (lane_group == g).astype(BF16)
-                lhs_s[n, 0, g * HALF : (g + 1) * HALF, :] = own_rows * keep
-            window = jnp.concatenate([turned_s[n], turned_s[n + 1]], axis=0)
-            big[n] = lax.dot_general(
-                lhs_s[n, 0], window, (((1,), (1,)), ((), ())), preferred_element_type=F32
+                lhs_s[slot, n, g * HALF : (g + 1) * HALF, :] = own_rows * keep
+            big[slot, n] = lax.dot_general(
+                lhs_s[slot, n],
+                mirrored[c, n * HALF : n * HALF + ROWS, :],
+                (((1,), (1,)), ((), ())),
+                preferred_element_type=F32,
             )
         for g in range(per_tile):
             rows = slice(g * HALF, (g + 1) * HALF)
             folded = jnp.zeros((HALF, LANES), F32)
             for n in range(2):
-                folded += big[n, rows, 0:LANES] * fmask32[n, 0]
-                folded += big[n, rows, LANES:] * fmask32[n, 1]
+                folded += big[slot, n, rows, 0:LANES] * fmask32[n, 0]
+                folded += big[slot, n, rows, LANES:] * fmask32[n, 1]
             turned = pltpu.roll(folded, 1, 1, stride=1, stride_axis=0)
-            red[c, g : g + 1, :] = jnp.sum(turned, axis=0, keepdims=True)
+            red_e[c, g : g + 1, :] = jnp.sum(turned, axis=0, keepdims=True)
+        red_e[c, 12:16, :] = jnp.zeros((4, LANES), F32)
+
+    def finish_rows(a, c, start, size):
+        w = wsc[c, a]
+        x = xf[a, c, 8 + start : 8 + start + size, :]
+        h0 = grads[a, c, start : start + size, :]
+        h1 = grads[a, c, start + 1 : start + 1 + size, :] * m1[start + 1 : start + 1 + size, :]
+        h2 = grads[a, c, start + 2 : start + 2 + size, :] * m2[start + 2 : start + 2 + size, :]
+        value = w[0:1] * h0 + w[1:2] * h1 + w[2:3] * h2
+        outs[a][start : start + size, cols(c)] = value.astype(BF16)
+        return [jnp.sum(h * x, axis=0, keepdims=True) for h in (h0, h1, h2)]
+
+    def finish_q(c, carry):
+        grads[0, c, ROWS : ROWS + 2, :] = tail_q_r[0:2, cols(c)]
+        parts = [finish_rows(0, c, start, HALF) for start in (0, HALF)]
+        for j in range(SHORT):
+            red_e[c, 9 + j : 10 + j, :] = parts[0][j] + parts[1][j]
         return carry
 
-    lax.fori_loop(0, nt, filter_sums, 0)
+    def finish_first(c, carry):
+        for a in (1, 2):
+            parts = finish_rows(a, c, 0, SPLIT)
+            for j in range(SHORT):
+                red_l[c, 3 * a - 3 + j : 3 * a - 2 + j, :] = parts[j]
+        red_l[c, 6:8, :] = jnp.zeros((2, LANES), F32)
+        return carry
+
+    def finish_last(c):
+        for a in (1, 2):
+            grads[a, c, ROWS : ROWS + 2, :] = tail_r[2 * a : 2 * a + 2, cols(c)]
+            parts = finish_rows(a, c, SPLIT, ROWS - SPLIT)
+            for j in range(SHORT):
+                red_l[c, 3 * a - 3 + j : 3 * a - 2 + j, :] += parts[j]
+
+    share = nt // ny
+
+    def tiles_of(at):
+        return pl.ds(at * share, share)
+
+    def to_owners(own, came, send, recv):
+        return [
+            remote(own.at[tiles_of(y_peer(d))], came.at[d], send.at[d], recv.at[d], (y_peer(d) * nz + z_at, tp))
+            for d in range(1, ny)
+        ]
+
+    def to_z(came, send, recv):
+        return [
+            remote(came.at[z_at], came.at[z_at], send.at[d], recv.at[d], (y_at * nz + z_peer(d), tp))
+            for d in range(1, nz)
+        ]
+
+    def to_y(whole, send, recv):
+        mine = whole.at[tiles_of(y_at)]
+        return [remote(mine, mine, send.at[d], recv.at[d], (y_peer(d) * nz + z_at, tp)) for d in range(1, ny)]
+
+    def launch(copies):
+        for copy in copies:
+            copy.start()
+
+    def add_owned(own, came, copies, target):
+        part = own[tiles_of(y_at)]
+        for d in range(1, ny):
+            copies[d - 1].wait_recv()
+            part = part + came[d]
+        target[z_at] = part
+
+    def add_z(came, send, recv, whole):
+        for d in range(1, nz):
+            slot = came.at[z_peer(nz - d)]
+            remote(slot, slot, send.at[d], recv.at[d], (y_at * nz + z_peer(d), tp)).wait_recv()
+        part = came[0]
+        for p in range(1, nz):
+            part = part + came[p]
+        whole[tiles_of(y_at)] = part * grad_scale
+
+    def wait_y(whole, send, recv):
+        for d in range(1, ny):
+            slot = whole.at[tiles_of(y_peer(ny - d))]
+            remote(slot, slot, send.at[d], recv.at[d], (y_peer(d) * nz + z_at, tp)).wait_recv()
+
+    tail_q.wait_recv()
+    lax.fori_loop(0, nt, finish_q, 0)
+    tiles(filter_sums)
+    e_owner = to_owners(red_e, e1, e1_send, e1_recv)
+    launch(e_owner)
+    lax.fori_loop(0, nt, finish_first, 0)
+    add_owned(red_e, e1, e_owner, e2)
+    e_z = to_z(e2, e2_send, e2_recv)
+    launch(e_z)
+    tail.wait_recv()
     backward_conv(1)
-    tail.wait_recv()
-
-    def finish(c, carry):
-        for a in range(3):
-            grads[a, c, ROWS : ROWS + 2, :] = tail_r[2 * a : 2 * a + 2, cols(c)]
-            w = wsc[c, a]
-            sums3 = [jnp.zeros((1, LANES), F32) for _ in range(SHORT)]
-            for start in (0, HALF):
-                x = xf[a, c, 8 + start : 8 + start + HALF, :]
-                h0 = grads[a, c, start : start + HALF, :]
-                h1 = grads[a, c, start + 1 : start + 1 + HALF, :] * m1[start + 1 : start + 1 + HALF, :]
-                h2 = grads[a, c, start + 2 : start + 2 + HALF, :] * m2[start + 2 : start + 2 + HALF, :]
-                value = w[0:1] * h0 + w[1:2] * h1 + w[2:3] * h2
-                outs[a][start : start + HALF, cols(c)] = value.astype(BF16)
-                for j, h in enumerate((h0, h1, h2)):
-                    sums3[j] += jnp.sum(h * x, axis=0, keepdims=True)
-            for j in range(SHORT):
-                at = 8 + 3 * a + j
-                red[c, at : at + 1, :] = sums3[j]
-        red[c, 18:24, :] = jnp.zeros((6, LANES), F32)
-        return carry
-
-    lax.fori_loop(0, nt, finish, 0)
-    sends_a = [
-        remote(red.at[z_peer(d)], red_a.at[d], ra_send.at[d], ra_recv.at[d], (y_at * nz + z_peer(d), tp))
-        for d in range(1, nz)
-    ]
-    for send in sends_a:
-        send.start()
-    part = red[z_at]
-    for d in range(1, nz):
-        sends_a[d - 1].wait_recv()
-        part = part + red_a[d]
-    red_b[y_at] = part
-    sends_b = [
-        remote(red_b.at[y_at], red_b.at[y_at], rb_send.at[d], rb_recv.at[d], (y_peer(d) * nz + z_at, tp))
-        for d in range(1, ny)
-    ]
-    for send in sends_b:
-        send.start()
-    for d in range(1, ny):
-        came = red_b.at[y_peer(ny - d)]
-        remote(came, came, rb_send.at[d], rb_recv.at[d], (y_peer(d) * nz + z_at, tp)).wait_recv()
-    whole = red_b[0]
-    for p in range(1, ny):
-        whole = whole + red_b[p]
-    fin[z_at] = whole * grad_scale
-    sends_c = [
-        remote(fin.at[z_at], fin.at[z_at], rc_send.at[d], rc_recv.at[d], (y_at * nz + z_peer(d), tp))
-        for d in range(1, nz)
-    ]
-    for send in sends_c:
-        send.start()
-    for d in range(1, nz):
-        came = fin.at[z_peer(nz - d)]
-        remote(came, came, rc_send.at[d], rc_recv.at[d], (y_at * nz + z_peer(d), tp)).wait_recv()
+    l_owner = to_owners(red_l, l1, l1_send, l1_recv)
+    launch(l_owner)
+    add_z(e2, e2_send, e2_recv, fin_e)
+    e_y = to_y(fin_e, e3_send, e3_recv)
+    launch(e_y)
+    add_owned(red_l, l1, l_owner, l2)
+    l_z = to_z(l2, l2_send, l2_recv)
+    launch(l_z)
+    wait_y(fin_e, e3_send, e3_recv)
     for c in range(nt):
         span = slice(c * LANES, (c + 1) * LANES)
-        filt_out[c * per_tile : (c + 1) * per_tile, :] = fin[c, 0:per_tile, :]
-        gain_out[:, span] = fin[c, 17:18, :]
-        for a in range(3):
-            short_out[a, :, span] = fin[c, 8 + 3 * a : 11 + 3 * a, :]
-
-    for copy in [doc_fwd, doc_bwd, edge, tail] + sends + sends_a + sends_b + sends_c:
+        filt_out[c * per_tile : (c + 1) * per_tile, :] = fin_e[c, 0:per_tile, :]
+        gain_out[:, span] = fin_e[c, 8:9, :]
+        short_out[0, :, span] = fin_e[c, 9:12, :]
+    add_z(l2, l2_send, l2_recv, fin_l)
+    l_y = to_y(fin_l, l3_send, l3_recv)
+    launch(l_y)
+    wait_y(fin_l, l3_send, l3_recv)
+    for c in range(nt):
+        span = slice(c * LANES, (c + 1) * LANES)
+        for a in (1, 2):
+            short_out[a, :, span] = fin_l[c, 3 * a - 3 : 3 * a, :]
+
+    for copy in [doc_fwd, doc_bwd, edge, tail_q, tail] + sends + e_owner + e_z + e_y + l_owner + l_z + l_y:
         copy.wait_send()
 
     def drain(c, carry):
@@ -568,17 +646,23 @@
             pltpu.VMEM((8, channels), F32),
             pltpu.VMEM((8, channels), F32),
             pltpu.VMEM((8, channels), F32),
+            pltpu.VMEM((8, channels), F32),
+            pltpu.VMEM((8, channels), F32),
             pltpu.VMEM((2, 2, HALF, LANES), F32),
             pltpu.VMEM((ntp, 8, LANES), F32),
             pltpu.VMEM((2, 2, HALF, LANES), F32),
-            pltpu.VMEM((2, 8 * HALF, 2 * LANES), F32),
+            pltpu.VMEM((2, 2, 8 * HALF, 2 * LANES), F32),
             pltpu.VMEM((2, 8 * HALF, LANES), F32),
             pltpu.VMEM((2, 2, 8 * HALF, LANES), BF16),
-            pltpu.VMEM((3, HALF, LANES), BF16),
-            pltpu.VMEM((nt, CHUNK, LANES), F32),
-            pltpu.VMEM((nz, CHUNK, LANES), F32),
-            pltpu.VMEM((ny, CHUNK, LANES), F32),
-            pltpu.VMEM((nz, CHUNK, LANES), F32),
+            pltpu.VMEM((nt, rows + HALF, LANES), BF16),
+            pltpu.VMEM((nt, 16, LANES), F32),
+            pltpu.VMEM((nt, 8, LANES), F32),
+            pltpu.VMEM((ny, nt // ny, 16, LANES), F32),
+            pltpu.VMEM((nz, nt // ny, 16, LANES), F32),
+            pltpu.VMEM((nt, 16, LANES), F32),
+            pltpu.VMEM((ny, nt // ny, 8, LANES), F32),
+            pltpu.VMEM((nz, nt // ny, 8, LANES), F32),
+            pltpu.VMEM((nt, 8, LANES), F32),
             dma((4,)),
             dma((4,)),
             dma((4,)),
@@ -588,12 +672,19 @@
             dma((nt,)),
             dma((ntp,)),
             dma((ntp,)),
+            dma((2,)),
+            dma((ny,)),
+            dma((ny,)),
             dma((nz,)),
             dma((nz,)),
             dma((ny,)),
             dma((ny,)),
+            dma((ny,)),
+            dma((ny,)),
             dma((nz,)),
             dma((nz,)),
+            dma((ny,)),
+            dma((ny,)),
         ],
         compiler_params=pltpu.CompilerParams(
             collective_id=0, has_side_effects=True, vmem_limit_bytes=60 * 1024 * 1024

time: 52.1 us -> 57.1 us (1.096)
  the two profiles are of different devices: /device:TPU:16 before, /device:TPU:2 now
where the time goes in v3:
time: 57.1 us; the launch traced here: 56.3 us
  Pallas kernels  55.7 us (98%)
  between operations  0.64 us (1%)
    pallas_call x1, Pallas kernels, on_device(): pl.pallas_call(functools.partial(kernel, ny, nz, ntp), name='mixer_backwa...  54.5 us
    pallas_call x1, Pallas kernels, on_device(): pl.pallas_call(publish, name='publish', out_shape=[jax.ShapeDtypeStruct(x...  1.21 us

profile of v3, /device:TPU:2, one launch (start us, length us, event | category | flops | bytes accessed | tf_op | source)
XLA Modules:
  0.0 56.3 jit_solution(12907004935591569978)
XLA Ops:
  0.6 54.5 %mixer_backward.1 = (bf16[256,1024]{1,0:T(8,128)(2,1)S(1)}, bf16[256,1024]{1,0:T(8,128)(2,1)S(1)}, bf16[256,1024]{1,0:T(8,128)(2,1)S(1)}, f32[1,1024]{1,0:T(1,12...) custom-call(bf16[256,1024]{1,0:T(8,128)(2,1)} %q_hbm.1, bf16[256,1024]{1,0:T(8,128)(2,1)} %k_hbm.1, ...), custom_call_target="tpu_custom_call" | custom-call | tf_op jit(solution)/shard_map/mixer_backward/pallas_call | solution.py:609
  55.1 1.2 %publish.1 = (bf16[256,1024]{1,0:T(8,128)(2,1)}, bf16[256,1024]{1,0:T(8,128)(2,1)}, bf16[256,1024]{1,0:T(8,128)(2,1)}, f32[1,1024]{1,0:T(1,128)}, f32[64,128]{1,0:T(8,128)}, /*index=5*/f32[3,3,1024]{2,1,0:T(4,128)}) custom-call(bf16[256,1024]{1,0:T(8,128)(2,1)S(1)} %get-tuple-element.18.refs_0_, bf16[256,1024]{1,0:T(8,128)(2,1)S(1)} %get-tuple-element.19.refs_1_, ...), custom_call_target="tpu_custom_call" | custom-call | tf_op jit(solution)/shard_map/publish/pallas_call | solution.py:702

commit v4 on v3

--- a/solution.py
+++ b/solution.py
@@ -17,7 +17,6 @@
 SHORT = 3
 EPS = 1e-06
 RING = 8
-SPLIT = 120
 
 
 def iota(axis):
@@ -47,16 +46,20 @@
     k_hbm,
     v_hbm,
     go_hbm,
-    docs_ref,
-    gain_ref,
-    filt_ref,
-    sw_ref,
+    docs_hbm,
+    gain_hbm,
+    filt_hbm,
+    sw_hbm,
     gq_ref,
     gk_ref,
     gv_ref,
     gain_out,
     filt_out,
     short_out,
+    docs_ref,
+    gain_ref,
+    filt_ref,
+    sw_ref,
     xin,
     go_v,
     xf,
@@ -79,6 +82,7 @@
     m2,
     docs_prev,
     docs_next,
+    edge_f,
     edge_s,
     edge_r,
     tail_s,
@@ -125,7 +129,7 @@
 ):
     nt = nz
     outs = (gq_ref, gk_ref, gv_ref)
-    groups = filt_ref.shape[0]
+    groups = filt_hbm.shape[0]
     per_tile = groups // nt
     width = LANES // per_tile
     n_ctx = ny * nz
@@ -159,7 +163,13 @@
         pltpu.make_async_copy(q_hbm, xin.at[0], load_sem.at[0]),
         pltpu.make_async_copy(go_hbm, go_v, load_sem.at[3]),
     ]
-    for load in loads:
+    small_loads = [
+        pltpu.make_async_copy(sw_hbm, sw_ref, load_sem.at[4]),
+        pltpu.make_async_copy(docs_hbm, docs_ref, load_sem.at[5]),
+        pltpu.make_async_copy(filt_hbm, filt_ref, load_sem.at[6]),
+        pltpu.make_async_copy(gain_hbm, gain_ref, load_sem.at[7]),
+    ]
+    for load in small_loads + loads:
         load.start()
 
     barrier = pltpu.get_barrier_semaphore()
@@ -170,6 +180,8 @@
     for where in partners:
         pl.semaphore_signal(barrier, inc=1, device_id=where, device_id_type=MESH)
 
+    for load in small_loads:
+        load.wait()
     for a in range(3):
         taps = sw_ref[a].astype(F32)
         for c in range(nt):
@@ -196,8 +208,9 @@
         load.wait()
     for a in range(3):
         last = xin[a, ROWS - 16 : ROWS, :].astype(F32)
-        edge_s[2 * a : 2 * a + 2, :] = last[14:16]
-    edge_s[6:8, :] = jnp.zeros((2, channels), F32)
+        edge_f[2 * a : 2 * a + 2, :] = last[14:16]
+    edge_f[6:8, :] = jnp.zeros((2, channels), F32)
+    edge_s[...] = edge_f[...].astype(BF16)
 
     doc_fwd = remote(docs_ref, docs_prev, doc_sem.at[0], doc_sem.at[1], (nxt, tp))
     doc_bwd = remote(docs_ref, docs_next, doc_sem.at[2], doc_sem.at[3], (prv, tp))
@@ -238,19 +251,14 @@
         for a in (1, 2):
             xf[a, c, 8 : 8 + ROWS, :] = xin[a, :, cols(c)].astype(F32)
         products(c, HALF)
+        halo1(c).start()
         return carry
 
-    lax.fori_loop(0, nt, late_half, 0)
     pl.semaphore_wait(barrier, len(partners))
     doc_fwd.start()
     doc_bwd.start()
     edge.start()
-
-    def send_product(c, carry):
-        halo1(c).start()
-        return carry
-
-    lax.fori_loop(0, nt, send_product, 0)
+    lax.fori_loop(0, nt, late_half, 0)
 
     def build(source, target):
         def one(c, carry):
@@ -293,16 +301,15 @@
         bmask[n, 0] = pick(j_at >= i_at, own_col[n], own[n]).astype(BF16)
         bmask[n, 1] = pick(j_at < i_at, own_col[n], after_rows[n]).astype(BF16)
 
-    def early_half(c, carry):
+    def early_half(c):
         xf[0, c, 8 : 8 + ROWS, :] = xin[0, :, cols(c)].astype(F32)
+        came = edge_r[:, cols(c)].astype(F32)
         for a in range(3):
-            xf[a, c, 6:8, :] = edge_r[2 * a : 2 * a + 2, cols(c)]
+            xf[a, c, 6:8, :] = came[2 * a : 2 * a + 2]
         products(c, 0)
         for start in (0, HALF):
             feats[0, c, start : start + HALF, :] = feature(0, c, start)
-        return carry
-
-    lax.fori_loop(0, nt, early_half, 0)
+
     loads[3].wait()
 
     lane_group = lax.div(iota(1), width)
@@ -345,6 +352,8 @@
         span = slice(n * HALF, (n + 1) * HALF)
 
         def one(c, slot):
+            if n == 1:
+                early_half(c)
             value = convolve(ring_f.at[c], fmask[n], prod[c, n * HALF : n * HALF + ROWS, :], slot)
             mixed[c, span, :] = value
             y = feats[0, c, span, :] * value
@@ -385,7 +394,7 @@
     def backward_norm(n):
         span = slice(n * HALF, (n + 1) * HALF)
 
-        def one(c, carry):
+        def one(c, carry=0):
             cot = go_v[span, cols(c)].astype(F32)
             y = y_s[c, span, :]
             row_scale = scales[n, 0]
@@ -403,26 +412,42 @@
                 tail_q_s[0:2, cols(c)] = grads[0, c, 0:2, :]
             return carry
 
-        lax.fori_loop(0, nt, one, 0)
+        return one
 
     tail_q_s[2:8, :] = jnp.zeros((6, channels), F32)
-    backward_norm(0)
+    first_norm = backward_norm(0)
+    lax.fori_loop(0, nt, first_norm, 0)
     tail_q = remote(tail_q_s, tail_q_r, tq_sem.at[0], tq_sem.at[1], (prv, tp))
     tail_q.start()
-    backward_norm(1)
+    last_norm = backward_norm(1)
+
+    def tap_sums(a, c, grad, start):
+        rows = slice(start, start + HALF)
+        shifted = [xf[a, c, 8 - j + start : 8 - j + start + HALF, :] for j in range(SHORT)]
+        terms = (grad * shifted[0], grad * m1[rows, :] * shifted[1], grad * m2[rows, :] * shifted[2])
+        return [jnp.sum(term, axis=0, keepdims=True) for term in terms]
 
     def backward_conv(n):
         span = slice(n * HALF, (n + 1) * HALF)
 
         def one(c, slot):
+            if n == 0:
+                last_norm(c)
             value = convolve(ring_b.at[c], bmask[n], gmix[c, n * HALF : n * HALF + ROWS, :], slot)
-            grads[1, c, span, :] = value * feats[2, c, span, :]
-            grads[2, c, span, :] = value * feats[1, c, span, :]
+            for a in (1, 2):
+                grad = value * feats[3 - a, c, span, :]
+                grads[a, c, span, :] = grad
+                parts = tap_sums(a, c, grad, n * HALF)
+                for j in range(SHORT):
+                    at = slice(3 * a - 3 + j, 3 * a - 2 + j)
+                    red_l[c, at, :] = parts[j] if n == 0 else red_l[c, at, :] + parts[j]
             if n == 0:
                 tail_s[2:4, cols(c)] = grads[1, c, 0:2, :]
                 tail_s[4:6, cols(c)] = grads[2, c, 0:2, :]
-            else:
-                finish_last(c)
+                red_l[c, 6:8, :] = jnp.zeros((2, LANES), F32)
+                parts = [tap_sums(0, c, grads[0, c, s : s + HALF, :], s) for s in (0, HALF)]
+                for j in range(SHORT):
+                    red_e[c, 9 + j : 10 + j, :] = parts[0][j] + parts[1][j]
 
         tiles(one, (lambda c: halo2(c).wait_recv()) if n == 1 else None)
 
@@ -454,37 +479,17 @@
             red_e[c, g : g + 1, :] = jnp.sum(turned, axis=0, keepdims=True)
         red_e[c, 12:16, :] = jnp.zeros((4, LANES), F32)
 
-    def finish_rows(a, c, start, size):
-        w = wsc[c, a]
-        x = xf[a, c, 8 + start : 8 + start + size, :]
-        h0 = grads[a, c, start : start + size, :]
-        h1 = grads[a, c, start + 1 : start + 1 + size, :] * m1[start + 1 : start + 1 + size, :]
-        h2 = grads[a, c, start + 2 : start + 2 + size, :] * m2[start + 2 : start + 2 + size, :]
-        value = w[0:1] * h0 + w[1:2] * h1 + w[2:3] * h2
-        outs[a][start : start + size, cols(c)] = value.astype(BF16)
-        return [jnp.sum(h * x, axis=0, keepdims=True) for h in (h0, h1, h2)]
-
-    def finish_q(c, carry):
-        grads[0, c, ROWS : ROWS + 2, :] = tail_q_r[0:2, cols(c)]
-        parts = [finish_rows(0, c, start, HALF) for start in (0, HALF)]
-        for j in range(SHORT):
-            red_e[c, 9 + j : 10 + j, :] = parts[0][j] + parts[1][j]
+    def write_grads(c, carry):
+        for a, came in enumerate((tail_q_r, tail_r, tail_r)):
+            grads[a, c, ROWS : ROWS + 2, :] = came[2 * a : 2 * a + 2, cols(c)]
+            w = wsc[c, a]
+            for start in (0, HALF):
+                h0, h1, h2 = [grads[a, c, start + j : start + j + HALF, :] for j in range(SHORT)]
+                h1 = h1 * m1[start + 1 : start + 1 + HALF, :]
+                h2 = h2 * m2[start + 2 : start + 2 + HALF, :]
+                value = w[0:1] * h0 + w[1:2] * h1 + w[2:3] * h2
+                outs[a][start : start + HALF, cols(c)] = value.astype(BF16)
         return carry
-
-    def finish_first(c, carry):
-        for a in (1, 2):
-            parts = finish_rows(a, c, 0, SPLIT)
-            for j in range(SHORT):
-                red_l[c, 3 * a - 3 + j : 3 * a - 2 + j, :] = parts[j]
-        red_l[c, 6:8, :] = jnp.zeros((2, LANES), F32)
-        return carry
-
-    def finish_last(c):
-        for a in (1, 2):
-            grads[a, c, ROWS : ROWS + 2, :] = tail_r[2 * a : 2 * a + 2, cols(c)]
-            parts = finish_rows(a, c, SPLIT, ROWS - SPLIT)
-            for j in range(SHORT):
-                red_l[c, 3 * a - 3 + j : 3 * a - 2 + j, :] += parts[j]
 
     share = nt // ny
 
@@ -532,34 +537,33 @@
             slot = whole.at[tiles_of(y_peer(ny - d))]
             remote(slot, slot, send.at[d], recv.at[d], (y_peer(d) * nz + z_at, tp)).wait_recv()
 
-    tail_q.wait_recv()
-    lax.fori_loop(0, nt, finish_q, 0)
     tiles(filter_sums)
     e_owner = to_owners(red_e, e1, e1_send, e1_recv)
     launch(e_owner)
-    lax.fori_loop(0, nt, finish_first, 0)
+    backward_conv(1)
+    l_owner = to_owners(red_l, l1, l1_send, l1_recv)
+    launch(l_owner)
     add_owned(red_e, e1, e_owner, e2)
     e_z = to_z(e2, e2_send, e2_recv)
     launch(e_z)
+    tail_q.wait_recv()
     tail.wait_recv()
-    backward_conv(1)
-    l_owner = to_owners(red_l, l1, l1_send, l1_recv)
-    launch(l_owner)
+    lax.fori_loop(0, nt, write_grads, 0)
+    add_owned(red_l, l1, l_owner, l2)
+    l_z = to_z(l2, l2_send, l2_recv)
+    launch(l_z)
     add_z(e2, e2_send, e2_recv, fin_e)
     e_y = to_y(fin_e, e3_send, e3_recv)
     launch(e_y)
-    add_owned(red_l, l1, l_owner, l2)
-    l_z = to_z(l2, l2_send, l2_recv)
-    launch(l_z)
+    add_z(l2, l2_send, l2_recv, fin_l)
+    l_y = to_y(fin_l, l3_send, l3_recv)
+    launch(l_y)
     wait_y(fin_e, e3_send, e3_recv)
     for c in range(nt):
         span = slice(c * LANES, (c + 1) * LANES)
         filt_out[c * per_tile : (c + 1) * per_tile, :] = fin_e[c, 0:per_tile, :]
         gain_out[:, span] = fin_e[c, 8:9, :]
         short_out[0, :, span] = fin_e[c, 9:12, :]
-    add_z(l2, l2_send, l2_recv, fin_l)
-    l_y = to_y(fin_l, l3_send, l3_recv)
-    launch(l_y)
     wait_y(fin_l, l3_send, l3_recv)
     for c in range(nt):
         span = slice(c * LANES, (c + 1) * LANES)
@@ -617,9 +621,13 @@
             resident((groups, taps), F32),
             resident((3, SHORT, channels), F32),
         ),
-        in_specs=[pl.BlockSpec(memory_space=pltpu.HBM)] * 4 + [vmem] * 4,
+        in_specs=[pl.BlockSpec(memory_space=pltpu.HBM)] * 8,
         out_specs=(vmem,) * 6,
         scratch_shapes=[
+            pltpu.VMEM((2, LANES), jnp.int32),
+            pltpu.VMEM((channels,), BF16),
+            pltpu.VMEM((groups, taps), BF16),
+            pltpu.VMEM((3, SHORT, channels), BF16),
             pltpu.VMEM((3, rows, channels), BF16),
             pltpu.VMEM((rows, channels), BF16),
             pltpu.VMEM((3, nt, rows + 8, LANES), F32),
@@ -643,7 +651,8 @@
             pltpu.VMEM((2, LANES), jnp.int32),
             pltpu.VMEM((2, LANES), jnp.int32),
             pltpu.VMEM((8, channels), F32),
-            pltpu.VMEM((8, channels), F32),
+            pltpu.VMEM((8, channels), BF16),
+            pltpu.VMEM((8, channels), BF16),
             pltpu.VMEM((8, channels), F32),
             pltpu.VMEM((8, channels), F32),
             pltpu.VMEM((8, channels), F32),
@@ -663,7 +672,7 @@
             pltpu.VMEM((ny, nt // ny, 8, LANES), F32),
             pltpu.VMEM((nz, nt // ny, 8, LANES), F32),
             pltpu.VMEM((nt, 8, LANES), F32),
-            dma((4,)),
+            dma((8,)),
             dma((4,)),
             dma((4,)),
             dma((nt,)),

time: 57.1 us -> 45.9 us (0.80)
  Pallas kernels: 55.7 us -> 44.5 us
    pallas_call x1, Pallas kernels: 54.5 us -> 43.3 us  [on_device(): pl.pallas_call(functools.partial(kernel, ny, nz, ntp), name='mixer_backwa...]
where the time goes in v4:
time: 45.9 us; the launch traced here: 45.1 us
  Pallas kernels  44.5 us (97%)
  between operations  0.64 us (1%)
    pallas_call x1, Pallas kernels, on_device(): pl.pallas_call(functools.partial(kernel, ny, nz, ntp), name='mixer_backwa...  43.3 us
    pallas_call x1, Pallas kernels, on_device(): pl.pallas_call(publish, name='publish', out_shape=[jax.ShapeDtypeStruct(x...  1.21 us

profile of v4, /device:TPU:2, one launch (start us, length us, event | category | flops | bytes accessed | tf_op | source)
XLA Modules:
  0.0 45.1 jit_solution(14195384753570818856)
XLA Ops:
  0.6 43.3 %mixer_backward.1 = (bf16[256,1024]{1,0:T(8,128)(2,1)S(1)}, bf16[256,1024]{1,0:T(8,128)(2,1)S(1)}, bf16[256,1024]{1,0:T(8,128)(2,1)S(1)}, f32[1,1024]{1,0:T(1,12...) custom-call(bf16[256,1024]{1,0:T(8,128)(2,1)} %q_hbm.1, bf16[256,1024]{1,0:T(8,128)(2,1)} %k_hbm.1, ...), custom_call_target="tpu_custom_call" | custom-call | tf_op jit(solution)/shard_map/mixer_backward/pallas_call | solution.py:613
  43.9 1.2 %publish.1 = (bf16[256,1024]{1,0:T(8,128)(2,1)}, bf16[256,1024]{1,0:T(8,128)(2,1)}, bf16[256,1024]{1,0:T(8,128)(2,1)}, f32[1,1024]{1,0:T(1,128)}, f32[64,128]{1,0:T(8,128)}, /*index=5*/f32[3,3,1024]{2,1,0:T(4,128)}) custom-call(bf16[256,1024]{1,0:T(8,128)(2,1)S(1)} %get-tuple-element.18.refs_0_, bf16[256,1024]{1,0:T(8,128)(2,1)S(1)} %get-tuple-element.19.refs_1_, ...), custom_call_target="tpu_custom_call" | custom-call | tf_op jit(solution)/shard_map/publish/pallas_call | solution.py:711

commit v5 on v4

--- a/solution.py
+++ b/solution.py
@@ -31,6 +31,10 @@
 
 def flip():
     return iota(0) + iota(1) == LANES - 1
+
+
+def far_first(count):
+    return sorted(range(1, count), key=lambda d: abs(2 * d - count))
 
 
 def mirror():
@@ -272,7 +276,6 @@
         lax.fori_loop(0, nt, one, 0)
 
     build(filt_rev, ring_f)
-    build(filt32, ring_b)
 
     doc_fwd.wait_recv()
     doc_bwd.wait_recv()
@@ -376,8 +379,9 @@
         remote(stats.at[tp], stats.at[tp], st_send.at[d], st_recv.at[d], (ctx, tp_peer(d)))
         for d in range(1, ntp)
     ]
-    for send in sends:
-        send.start()
+    for d in far_first(ntp):
+        sends[d - 1].start()
+    build(filt32, ring_b)
     lax.fori_loop(0, nt, mirror_products, 0)
     for d in range(1, ntp):
         came = stats.at[tp_peer(ntp - d)]
@@ -513,8 +517,8 @@
         return [remote(mine, mine, send.at[d], recv.at[d], (y_peer(d) * nz + z_at, tp)) for d in range(1, ny)]
 
     def launch(copies):
-        for copy in copies:
-            copy.start()
+        for d in far_first(len(copies) + 1):
+            copies[d - 1].start()
 
     def add_owned(own, came, copies, target):
         part = own[tiles_of(y_at)]
@@ -564,21 +568,23 @@
         filt_out[c * per_tile : (c + 1) * per_tile, :] = fin_e[c, 0:per_tile, :]
         gain_out[:, span] = fin_e[c, 8:9, :]
         short_out[0, :, span] = fin_e[c, 9:12, :]
+    for copy in [doc_fwd, doc_bwd, edge, tail_q, tail] + sends + e_owner + e_z + e_y + l_owner + l_z:
+        copy.wait_send()
+
+    def drain(c, carry):
+        halo1(c).wait_send()
+        halo2(c).wait_send()
+        return carry
+
+    lax.fori_loop(0, nt, drain, 0)
     wait_y(fin_l, l3_send, l3_recv)
     for c in range(nt):
         span = slice(c * LANES, (c + 1) * LANES)
         for a in (1, 2):
             short_out[a, :, span] = fin_l[c, 3 * a - 3 : 3 * a, :]
 
-    for copy in [doc_fwd, doc_bwd, edge, tail_q, tail] + sends + e_owner + e_z + e_y + l_owner + l_z + l_y:
+    for copy in l_y:
         copy.wait_send()
-
-    def drain(c, carry):
-        halo1(c).wait_send()
-        halo2(c).wait_send()
-        return carry
-
-    lax.fori_loop(0, nt, drain, 0)
 
 
 def resident(shape, dtype):

time: 45.9 us -> 45.3 us (0.987); the launches traced: 45.1 us -> 45 us
  no operation moved by 1% of the time
where the time goes in v5:
time: 45.3 us; the launch traced here: 45 us
  Pallas kernels  44.4 us (98%)
  between operations  0.64 us (1%)
    pallas_call x1, Pallas kernels, on_device(): pl.pallas_call(functools.partial(kernel, ny, nz, ntp), name='mixer_backwa...  43.2 us
    pallas_call x1, Pallas kernels, on_device(): pl.pallas_call(publish, name='publish', out_shape=[jax.ShapeDtypeStruct(x...  1.21 us

profile of v5, /device:TPU:2, one launch (start us, length us, event | category | flops | bytes accessed | tf_op | source)
XLA Modules:
  0.0 45.0 jit_solution(14877762821382511529)
XLA Ops:
  0.6 43.2 %mixer_backward.1 = (bf16[256,1024]{1,0:T(8,128)(2,1)S(1)}, bf16[256,1024]{1,0:T(8,128)(2,1)S(1)}, bf16[256,1024]{1,0:T(8,128)(2,1)S(1)}, f32[1,1024]{1,0:T(1,12...) custom-call(bf16[256,1024]{1,0:T(8,128)(2,1)} %q_hbm.1, bf16[256,1024]{1,0:T(8,128)(2,1)} %k_hbm.1, ...), custom_call_target="tpu_custom_call" | custom-call | tf_op jit(solution)/shard_map/mixer_backward/pallas_call | solution.py:619
  43.8 1.2 %publish.1 = (bf16[256,1024]{1,0:T(8,128)(2,1)}, bf16[256,1024]{1,0:T(8,128)(2,1)}, bf16[256,1024]{1,0:T(8,128)(2,1)}, f32[1,1024]{1,0:T(1,128)}, f32[64,128]{1,0:T(8,128)}, /*index=5*/f32[3,3,1024]{2,1,0:T(4,128)}) custom-call(bf16[256,1024]{1,0:T(8,128)(2,1)S(1)} %get-tuple-element.18.refs_0_, bf16[256,1024]{1,0:T(8,128)(2,1)S(1)} %get-tuple-element.19.refs_1_, ...), custom_call_target="tpu_custom_call" | custom-call | tf_op jit(solution)/shard_map/publish/pallas_call | solution.py:717
